TPU v7x, 256 devices: a whole 4x4x8 slice. The times are simulated.
256 devices in a mesh: gx: 16 (over z, core), gy: 16 (over x, y).
Axes of the slice: x: 4, y: 4, z: 8, core: 2. Of those that a mesh axis runs over, the one named last changes fastest.
Arguments:
- features: bfloat16 [256, 256, 1, 1024], P('gx', 'gy'), may hold values from -6 to 6
- slot_map: int32 [16, 16, 2], replicated, may hold values from -1 to 0, as said below
- tap_weights: float32 [27, 64], replicated, may hold values from -1.25 to 1.25
- gain: float32 [64], replicated, may hold values from 0.5 to 1.5
- mix_weight: bfloat16 [64, 64], replicated, may hold values from -0.75 to 0.75
- cotangent: bfloat16 [256, 256, 1, 1024], P('gx', 'gy'), may hold values from -6 to 6
Outputs:
- mixed: bfloat16 [256, 256, 1, 1024], P('gx', 'gy')
- grad_features: bfloat16 [256, 256, 1, 1024], P('gx', 'gy')
- grad_taps: float32 [27, 64], replicated
- grad_gain: float32 [64], replicated
- grad_mix: float32 [64, 64], replicated
Inputs may be any that keep to these rules, and one draw needn't show every extreme that they name: `slot_map`: in each block column the active levels carry slot numbers 0, 1, 2, ... in increasing level order and the others carry -1; every block column has exactly 1 active block.
All inputs are finite; a program needn't handle non-finite values.
Results may differ from a plain program's by a relative error of at most 0.0039.
Values may be sent and summed in bfloat16 or wider, within the bound.
A program may use at most 128 MiB of HBM per device.

v0:
```python
import jax
import jax.numpy as jnp
from jax import lax
from jax.sharding import PartitionSpec as P

EPS = 1e-05


def extended_2(cells, sides, width):
    for axis, dim in sides:
        count = lax.axis_size(axis)
        ends = count - 1
        head = lax.slice_in_dim(cells, 0, width, axis=dim)
        tail = lax.slice_in_dim(cells, cells.shape[dim] - width, cells.shape[dim], axis=dim)
        cells = jnp.concatenate(
            [
                lax.ppermute(tail, axis, [(i, (i + 1) % count) for i in range(ends)]),
                cells,
                lax.ppermute(head, axis, [((i + 1) % count, i) for i in range(ends)]),
            ],
            axis=dim,
        )
    return cells


def one_hot_map(level_slots, slot_count):
    slot_ids = jnp.arange(slot_count, dtype=jnp.int32)
    return (level_slots[..., None] == slot_ids).astype(jnp.bfloat16)


def slot_lookup(center, slot_count):
    slot_ids = jnp.arange(slot_count, dtype=jnp.int32)
    matches = center[:, None] == slot_ids[None, :]
    level_ids = jnp.arange(center.shape[0], dtype=jnp.int32)[:, None]
    position = jnp.sum(jnp.where(matches, level_ids, 0), axis=0)
    active = jnp.any(matches, axis=0)
    return (position, active)


def slot_slabs(extended, position, active, channels):
    levels = extended.shape[2]
    level_pad = jnp.pad(extended, ((0, 0), (0, 0), (1, 1), (0, 0)))
    level_ids = jnp.arange(levels + 2, dtype=jnp.int32)
    wanted = position[:, None] + jnp.arange(3, dtype=jnp.int32)[None, :]
    select = (wanted[:, :, None] == level_ids[None, None, :]) & active[:, None, None]
    picked = jnp.einsum(
        "xypf,skp->xyskf",
        level_pad,
        select.astype(jnp.bfloat16),
        preferred_element_type=jnp.float32,
    ).astype(jnp.bfloat16)
    below = picked[:, :, :, 0, -channels:]
    middle = picked[:, :, :, 1, :]
    above = picked[:, :, :, 2, :channels]
    return jnp.concatenate([below, middle, above], axis=-1)


def stencil(padded, taps):
    channels = taps.shape[1]
    inner = padded.shape[0] - 2
    length = padded.shape[-1] - 2 * channels
    accum_sum = jnp.zeros((inner, inner) + padded.shape[2:-1] + (length,), jnp.float32)
    for tap_index in range(27):
        off_x = tap_index // 9
        off_y = tap_index // 3 % 3
        off_z = tap_index % 3
        shifted = padded[
            off_x : off_x + inner,
            off_y : off_y + inner,
            ...,
            channels * off_z : channels * off_z + length,
        ].astype(jnp.float32)
        accum_sum = accum_sum + shifted * jnp.tile(taps[tap_index], length // channels)
    return accum_sum


def tap_grads(padded, grads, channels):
    inner = padded.shape[0] - 2
    length = padded.shape[-1] - 2 * channels
    rows_out = []
    for tap_index in range(27):
        off_x = tap_index // 9
        off_y = tap_index // 3 % 3
        off_z = tap_index % 3
        shifted = padded[
            off_x : off_x + inner,
            off_y : off_y + inner,
            ...,
            channels * off_z : channels * off_z + length,
        ].astype(jnp.float32)
        rows_out.append(jnp.sum((shifted * grads).reshape(-1, channels), axis=0))
    return jnp.stack(rows_out)


def norm_forward(depth_slots):
    mean_square = jnp.mean(depth_slots * depth_slots, axis=-1, keepdims=True)
    inv_rms = lax.rsqrt(mean_square + EPS)
    return (depth_slots * inv_rms, inv_rms)


def norm_backward(grad_norm, normed, inv_rms, gain):
    grad_scaled = grad_norm * gain
    return inv_rms * (grad_scaled - normed * jnp.mean(grad_scaled * normed, axis=-1, keepdims=True))


def shards(features, slot_map, tap_weights, gain, mix_weight, cotangent):
    block_side = features.shape[0]
    slot_count = features.shape[2]
    lane_width = features.shape[3]
    channels = gain.shape[0]
    depth_cells = lane_width // channels
    levels = slot_map.shape[2]
    cell_shape = (block_side, block_side, slot_count, depth_cells, channels)
    grid_row = lax.axis_index("gx")
    grid_col = lax.axis_index("gy")
    padded_map = jnp.pad(slot_map, ((1, 1), (1, 1), (0, 0)), constant_values=-1)
    near_maps = lax.dynamic_slice(padded_map, (grid_row, grid_col, jnp.int32(0)), (3, 3, levels))
    center = near_maps[1, 1]
    position, active = slot_lookup(center, slot_count)
    keep_mask = active.astype(jnp.float32)[None, None, :, None, None]

    def extend(slot_data):
        dense_field = jnp.einsum(
            "xysf,ps->xypf",
            slot_data,
            one_hot_map(center, slot_count),
            preferred_element_type=jnp.float32,
        ).astype(jnp.bfloat16)
        extended = extended_2(dense_field, (("gx", 0), ("gy", 1)), 1)
        return slot_slabs(extended, position, active, channels)

    padded_in = extend(features)
    depth_slots = stencil(padded_in, tap_weights).reshape(cell_shape)
    normed, inv_rms = norm_forward(depth_slots)
    norm_bf = (normed * gain).astype(jnp.bfloat16)
    branch = jnp.einsum("xyszc,cd->xyszd", norm_bf, mix_weight, preferred_element_type=jnp.float32)
    mixed = (
        ((features.reshape(cell_shape).astype(jnp.float32) + branch) * keep_mask)
        .astype(jnp.bfloat16)
        .reshape(features.shape)
    )
    grad_out = cotangent.reshape(cell_shape) * keep_mask.astype(jnp.bfloat16)
    grad_mix_part = jnp.einsum(
        "xyszc,xyszd->cd", norm_bf, grad_out, preferred_element_type=jnp.float32
    )
    grad_norm = jnp.einsum(
        "xyszd,cd->xyszc", grad_out, mix_weight, preferred_element_type=jnp.float32
    )
    grad_gain_part = jnp.sum(grad_norm * normed, axis=(0, 1, 2, 3))
    grad_depth = (
        (norm_backward(grad_norm, normed, inv_rms, gain) * keep_mask)
        .astype(jnp.bfloat16)
        .reshape(features.shape)
    )
    padded_grad = extend(grad_depth)
    back_slots = stencil(padded_grad, tap_weights[::-1])
    grad_features = (
        ((cotangent.astype(jnp.float32) + back_slots).reshape(cell_shape) * keep_mask)
        .astype(jnp.bfloat16)
        .reshape(features.shape)
    )
    grad_center = padded_grad[1:-1, 1:-1, :, channels:-channels].astype(jnp.float32)
    grad_taps_part = tap_grads(padded_in, grad_center, channels)
    grad_taps, grad_mix, grad_gain = lax.psum(
        (grad_taps_part, grad_mix_part, grad_gain_part), ("gx", "gy")
    )
    return (mixed, grad_features, grad_taps, grad_gain, grad_mix)


def solution(mesh):
    return jax.shard_map(
        shards,
        mesh=mesh,
        in_specs=(P("gx", "gy", None, None), P(), P(), P(), P(), P("gx", "gy", None, None)),
        out_specs=(P("gx", "gy", None, None), P("gx", "gy", None, None), P(), P(), P()),
        check_vma=False,
    )
```

profile of v0, /device:TPU:1, one launch (start us, length us, event | category | flops | bytes accessed | tf_op | source)
XLA Modules:
  0.0 338.6 jit_solution(7447671005226463131)
XLA Ops:
  4.5 5.1 %collective-permute-start = (bf16[1,16,2,1024]{3,2,1,0:T(2,128)(2,1)S(1)}, bf16[1,16,2,1024]{3,2,1,0:T(2,128)(2,1)S(1)}, u32[]{:S(2)}, u32[]{:S(2)}) collective-permute-start(bf16[1,16,2,1024]{3,2,1,0:T(2,128)(2,1)S(1)} %get-tuple-element.75), channel_id=1, source_target_pairs={{0,16},{16,32},{32,48},{48,64},{64,80},{80,96},{96,112},{112,128},... | collective-permute-start | bytes 196616 | tf_op jit(solution)/shard_map/ppermute | solution.py:17
  19.4 3.2 collective-permute-start.2
  24.8 2.9 collective-permute-done.3
  27.8 4.5 %convert_bitcast_fusion.1 = bf16[18,18,1,3,1024]{4,3,1,0,2:T(4,128)(2,1)S(1)} fusion(bf16[18,1,2,1024]{3,2,1,0:T(2,128)(2,1)S(1)} %collective-permute-done.3, bf16[18,1,2,1024]{3,2,1,0:T(2,128)(2,1)S(1)} %collective-permute-done.2, bf16[1,16,2,1024]{3,2,1,0:T(2,128)(2,1)S(1)} %collective-permute-done.1, bf16[16,16,2,1024]{3,2,1,0:T(2,128)(2,1)S(1)} %fusion.52, ...), kind=kOutput, calls=%fused_computation.88 | convolution fusion | flops 32845848 | bytes 3317773 | tf_op jit(solution)/shard_map/xypf,skp->xyskf/dot_general | solution.py:46
  34.6 9.4 %fusion.125 = (f32[16,16,1,1024]{3,1,0,2:T(8,128)}, f32[16,16,1,1024]{3,1,0,2:T(8,128)}) fusion(f32[1024]{0:T(1024)S(1)} %mul.720, bf16[18,18,1,64]{3,1,0,2:T(8,128)(2,1)S(1)} %get-tuple-element.105, bf16[18,18,1,1024]{3,1,0,2:T(8,128)(2,1)S(1)} %bitcast.278, f32[1024]{0:T(1024)S(1)} %mul.717, f32[1024]{0:T(1024)S(1)} %mul.714, ...), kind=kLoop, calls=%fused_computation.308 | loop fusion | flops 35389440 | bytes 8032256 | tf_op jit(solution)/shard_map/mul | solution.py:96
  52.8 3.1 multiply_convert_fusion.2
  65.5 5.1 %collective-permute-start.4 = (bf16[1,16,2,1024]{3,2,1,0:T(2,128)(2,1)}, bf16[1,16,2,1024]{3,2,1,0:T(2,128)(2,1)}, u32[]{:S(2)}, u32[]{:S(2)}) collective-permute-start(bf16[1,16,2,1024]{3,2,1,0:T(2,128)(2,1)} %get-tuple-element.73), channel_id=1, source_target_pairs={{0,16},{16,32},{32,48},{48,64},{64,80},{80,96},{96,112},{112,128},... | collective-permute-start | bytes 196616 | tf_op jit(solution)/shard_map/ppermute | solution.py:17
  77.3 3.2 collective-permute-start.6
  83.5 3.0 reshape.456
  86.6 5.0 %convert_bitcast_fusion = bf16[18,18,1,3,1024]{4,3,1,0,2:T(4,128)(2,1)S(1)} fusion(bf16[18,1,2,1024]{3,2,1,0:T(2,128)(2,1)S(1)} %collective-permute-done.7, bf16[18,1,2,1024]{3,2,1,0:T(2,128)(2,1)S(1)} %collective-permute-done.6, bf16[1,16,2,1024]{3,2,1,0:T(2,128)(2,1)} %collective-permute-done.5, bf16[16,16,2,1024]{3,2,1,0:T(2,128)(2,1)S(1)} %fusion.54, ...), kind=kOutput, calls=%fused_computation.87 | convolution fusion | flops 32845848 | bytes 3317773 | tf_op jit(solution)/shard_map/xypf,skp->xyskf/dot_general | solution.py:46
  93.8 4.0 %convert_multiply_fusion.2 = (f32[16,16,1,1024]{3,1,0,2:T(8,128)}, f32[16,16,1,1024]{3,1,0,2:T(8,128)}, f32[16,16,1,1024]{3,1,0,2:T(8,128)}, f32[16,16,1,1024]{3...) fusion(bf16[18,18,1,1024]{3,1,0,2:T(8,128)(2,1)S(1)} %bitcast.279, ...), kind=kLoop, calls=%fused_computation.2 | loop fusion | flops 8126464 | bytes 7520768 | tf_op jit(solution)/shard_map/mul | solution.py:91
  97.7 4.4 %convert_multiply_fusion.3 = (f32[16,16,1,1024]{3,1,0,2:T(8,128)}, f32[16,16,1,1024]{3,1,0,2:T(8,128)}, f32[16,16,1,1024]{3,1,0,2:T(8,128)}, f32[16,16,1,1024]{3...) fusion(bf16[18,18,1,64]{3,1,0,2:T(8,128)(2,1)S(1)} %copy-done.10, ...), kind=kLoop, calls=%fused_computation.3 | loop fusion | flops 8126464 | bytes 7562240 | tf_op jit(solution)/shard_map/mul | solution.py:91
  102.2 4.3 %convert_multiply_fusion = (f32[16,16,1,1024]{3,1,0,2:T(8,128)}, f32[16,16,1,1024]{3,1,0,2:T(8,128)}, f32[16,16,1,1024]{3,1,0,2:T(8,128)}, f32[16,16,1,1024]{3,1...) fusion(bf16[18,18,1,64]{3,1,0,2:T(8,128)(2,1)S(1)} %copy-done.10, ...), kind=kLoop, calls=%fused_computation | loop fusion | flops 8126464 | bytes 7520768 | tf_op jit(solution)/shard_map/mul | solution.py:91
  106.4 4.0 %convert_multiply_fusion.1 = (f32[16,16,1,1024]{3,1,0,2:T(8,128)}, f32[16,16,1,1024]{3,1,0,2:T(8,128)}, f32[16,16,1,1024]{3,1,0,2:T(8,128)}, f32[16,16,1,1024]{3...) fusion(bf16[18,18,1,1024]{3,1,0,2:T(8,128)(2,1)S(1)} %bitcast.2, ...), kind=kLoop, calls=%fused_computation.1 | loop fusion | flops 4980736 | bytes 14680064 | tf_op jit(solution)/shard_map/mul | solution.py:91
  110.4 2.9 reshape.482
  115.4 2.8 reshape.458
  120.4 3.0 reshape.461
  125.6 2.8 reshape.464
  130.6 2.8 reshape.467
  135.6 2.8 reshape.470
  140.6 2.8 reshape.481
  155.6 2.8 reshape.476
  160.6 2.8 reshape.473
  165.6 2.8 reshape.479
  170.6 2.8 reshape.484
  185.5 3.1 reshape.466
  190.7 2.8 reshape.469
  205.7 2.8 reshape.480
  210.7 2.8 reshape.477
  215.7 2.8 reshape.474
  245.2 9.3 %fusion.106 = bf16[16,16,1,1024]{3,1,2,0:T(8,128)(2,1)} fusion(f32[]{:T(128)S(6)} %convert_element_type.307, f32[1024]{0:T(1024)S(1)} %copy-done.14, bf16[18,18,1,64]{3,1,0,2:T(8,128)(2,1)S(1)} %bitcast.290, bf16[18,18,1,1024]{3,1,0,2:T(8,128)(2,1)S(1)} %bitcast.287, f32[1024]{0:T(1024)S(1)} %mul.645, f32[1024]{0:T(1024)S(1)} %mul.648, ...), kind=kLoop, calls=%fused_computation.245 | loop fusion | flops 36175872 | bytes 6983684
  254.5 83.8 %all-reduce.3 = (f32[27,64]{1,0:T(8,128)}, f32[64]{0:T(128)}, f32[64,64]{1,0:T(8,128)}) all-reduce(f32[27,64]{1,0:T(8,128)S(1)} %stack.111, f32[64]{0:T(128)S(1)} %copy-done.54, f32[64,64]{1,0:T(8,128)S(1)} %convolution_bitcast_fusion), channel_id=1, replica_groups=mesh['gx'=16,'gy'=16] {'gx','gy'}, use_global_device_ids=true, to_apply=%region_31.32 | all-reduce | flops 5888 | bytes 47104 | tf_op jit(solution)/shard_map/psum | solution.py:164
  (258 shorter events, 135.9 us)
Async XLA Ops:
  0.6 52.2 %copy-start = (bf16[64,64]{1,0:T(8,128)(2,1)S(1)}, bf16[64,64]{1,0:T(8,128)(2,1)}, u32[]{:S(2)}) copy-start(bf16[64,64]{1,0:T(8,128)(2,1)} %param.10) | copy-start | bytes 24580
  4.4 12.5 %copy-start.7 = (bf16[16,16,1,1024]{3,1,2,0:T(8,128)(2,1)S(1)}, bf16[16,16,1,1024]{3,1,2,0:T(8,128)(2,1)}, u32[]{:S(2)}) copy-start(bf16[16,16,1,1024]{3,1,2,0:T(8,128)(2,1)} %param.11) | copy-start | bytes 1572868
  4.5 14.7 %collective-permute-start = (bf16[1,16,2,1024]{3,2,1,0:T(2,128)(2,1)S(1)}, bf16[1,16,2,1024]{3,2,1,0:T(2,128)(2,1)S(1)}, u32[]{:S(2)}, u32[]{:S(2)}) collective-permute-start(bf16[1,16,2,1024]{3,2,1,0:T(2,128)(2,1)S(1)} %get-tuple-element.75), channel_id=1, source_target_pairs={{0,16},{16,32},{32,48},{48,64},{64,80},{80,96},{96,112},{112,128},... | collective-permute-start | bytes 196616 | tf_op jit(solution)/shard_map/ppermute | solution.py:17
  9.6 9.6 %collective-permute-start.1 = (bf16[1,16,2,1024]{3,2,1,0:T(2,128)(2,1)S(1)}, bf16[1,16,2,1024]{3,2,1,0:T(2,128)(2,1)S(1)}, u32[]{:S(2)}, u32[]{:S(2)}) collective-permute-start(bf16[1,16,2,1024]{3,2,1,0:T(2,128)(2,1)S(1)} %get-tuple-element.76), channel_id=1, source_target_pairs={{16,0},{32,16},{48,32},{64,48},{80,64},{96,80},{112,96},{128,112},... | collective-permute-start | bytes 196616 | tf_op jit(solution)/shard_map/ppermute | solution.py:19
  15.5 18.9 %copy-start.13 = (f32[1024]{0:T(1024)}, f32[1024]{0:T(1024)S(1)}, u32[]{:S(2)}) copy-start(f32[1024]{0:T(1024)S(1)} %mul.642) | copy-start | bytes 12292
  15.6 18.9 %copy-start.15 = (f32[1024]{0:T(1024)}, f32[1024]{0:T(1024)S(1)}, u32[]{:S(2)}) copy-start(f32[1024]{0:T(1024)S(1)} %mul.714) | copy-start | bytes 12292
  15.7 18.8 %copy-start.17 = (f32[1024]{0:T(1024)}, f32[1024]{0:T(1024)S(1)}, u32[]{:S(2)}) copy-start(f32[1024]{0:T(1024)S(1)} %mul.711) | copy-start | bytes 12292
  15.7 18.7 %copy-start.19 = (f32[1024]{0:T(1024)}, f32[1024]{0:T(1024)S(1)}, u32[]{:S(2)}) copy-start(f32[1024]{0:T(1024)S(1)} %mul.708) | copy-start | bytes 12292
  15.8 18.7 %copy-start.21 = (f32[1024]{0:T(1024)}, f32[1024]{0:T(1024)S(1)}, u32[]{:S(2)}) copy-start(f32[1024]{0:T(1024)S(1)} %mul.705) | copy-start | bytes 12292
  15.9 18.6 %copy-start.23 = (f32[1024]{0:T(1024)}, f32[1024]{0:T(1024)S(1)}, u32[]{:S(2)}) copy-start(f32[1024]{0:T(1024)S(1)} %mul.702) | copy-start | bytes 12292
  16.0 18.5 %copy-start.25 = (f32[1024]{0:T(1024)}, f32[1024]{0:T(1024)S(1)}, u32[]{:S(2)}) copy-start(f32[1024]{0:T(1024)S(1)} %mul.699) | copy-start | bytes 12292
  16.0 18.5 %copy-start.27 = (f32[1024]{0:T(1024)}, f32[1024]{0:T(1024)S(1)}, u32[]{:S(2)}) copy-start(f32[1024]{0:T(1024)S(1)} %mul.696) | copy-start | bytes 12292
  16.1 18.4 %copy-start.29 = (f32[1024]{0:T(1024)}, f32[1024]{0:T(1024)S(1)}, u32[]{:S(2)}) copy-start(f32[1024]{0:T(1024)S(1)} %mul.693) | copy-start | bytes 12292
  16.2 18.3 %copy-start.31 = (f32[1024]{0:T(1024)}, f32[1024]{0:T(1024)S(1)}, u32[]{:S(2)}) copy-start(f32[1024]{0:T(1024)S(1)} %mul.690) | copy-start | bytes 12292
  16.3 18.3 %copy-start.33 = (f32[1024]{0:T(1024)}, f32[1024]{0:T(1024)S(1)}, u32[]{:S(2)}) copy-start(f32[1024]{0:T(1024)S(1)} %mul.687) | copy-start | bytes 12292
  16.4 18.2 %copy-start.35 = (f32[1024]{0:T(1024)}, f32[1024]{0:T(1024)S(1)}, u32[]{:S(2)}) copy-start(f32[1024]{0:T(1024)S(1)} %mul.684) | copy-start | bytes 12292
  16.4 18.1 %copy-start.37 = (f32[1024]{0:T(1024)}, f32[1024]{0:T(1024)S(1)}, u32[]{:S(2)}) copy-start(f32[1024]{0:T(1024)S(1)} %mul.681) | copy-start | bytes 12292
  16.5 18.1 %copy-start.39 = (f32[1024]{0:T(1024)}, f32[1024]{0:T(1024)S(1)}, u32[]{:S(2)}) copy-start(f32[1024]{0:T(1024)S(1)} %mul.678) | copy-start | bytes 12292
  16.6 18.0 %copy-start.41 = (f32[1024]{0:T(1024)}, f32[1024]{0:T(1024)S(1)}, u32[]{:S(2)}) copy-start(f32[1024]{0:T(1024)S(1)} %mul.675) | copy-start | bytes 12292
  16.7 17.9 %copy-start.43 = (f32[1024]{0:T(1024)}, f32[1024]{0:T(1024)S(1)}, u32[]{:S(2)}) copy-start(f32[1024]{0:T(1024)S(1)} %mul.672) | copy-start | bytes 12292
  16.7 17.9 %copy-start.45 = (f32[1024]{0:T(1024)}, f32[1024]{0:T(1024)S(1)}, u32[]{:S(2)}) copy-start(f32[1024]{0:T(1024)S(1)} %mul.669) | copy-start | bytes 12292
  16.8 17.8 %copy-start.47 = (f32[1024]{0:T(1024)}, f32[1024]{0:T(1024)S(1)}, u32[]{:S(2)}) copy-start(f32[1024]{0:T(1024)S(1)} %mul.666) | copy-start | bytes 12292
  16.9 17.7 %copy-start.49 = (f32[1024]{0:T(1024)}, f32[1024]{0:T(1024)S(1)}, u32[]{:S(2)}) copy-start(f32[1024]{0:T(1024)S(1)} %mul.663) | copy-start | bytes 12292
  19.4 5.4 %collective-permute-start.2 = (bf16[18,1,2,1024]{3,2,1,0:T(2,128)(2,1)S(1)}, bf16[18,1,2,1024]{3,2,1,0:T(2,128)(2,1)S(1)}, u32[]{:S(2)}, u32[]{:S(2)}) collective-permute-start(bf16[18,1,2,1024]{3,2,1,0:T(2,128)(2,1)S(1)} %get-tuple-element.71), channel_id=1, source_target_pairs={{0,1},{1,2},{2,3},{3,4},{4,5},{5,6},{6,7},{7,8},{8,9},{9,10},{10,1... | collective-permute-start | bytes 221192 | tf_op jit(solution)/shard_map/ppermute | solution.py:17
  22.7 5.1 %collective-permute-start.3 = (bf16[18,1,2,1024]{3,2,1,0:T(2,128)(2,1)S(1)}, bf16[18,1,2,1024]{3,2,1,0:T(2,128)(2,1)S(1)}, u32[]{:S(2)}, u32[]{:S(2)}) collective-permute-start(bf16[18,1,2,1024]{3,2,1,0:T(2,128)(2,1)S(1)} %get-tuple-element.72), channel_id=1, source_target_pairs={{1,0},{2,1},{3,2},{4,3},{5,4},{6,5},{7,6},{8,7},{9,8},{10,9},{11,1... | collective-permute-start | bytes 221192 | tf_op jit(solution)/shard_map/ppermute | solution.py:19
  59.6 12.8 %copy-start.2 = (f32[16,16,1,1024]{3,1,0,2:T(8,128)S(1)}, f32[16,16,1,1024]{3,1,0,2:T(8,128)}, u32[]{:S(2)}) copy-start(f32[16,16,1,1024]{3,1,0,2:T(8,128)} %get-tuple-element.33) | copy-start | bytes 3145732
  59.6 12.8 %copy-start.51 = (f32[1024]{0:T(1024)S(1)}, f32[1024]{0:T(1024)}, u32[]{:S(2)}) copy-start(f32[1024]{0:T(1024)} %mul.800) | copy-start | bytes 12292
  65.5 8.9 %collective-permute-start.4 = (bf16[1,16,2,1024]{3,2,1,0:T(2,128)(2,1)}, bf16[1,16,2,1024]{3,2,1,0:T(2,128)(2,1)}, u32[]{:S(2)}, u32[]{:S(2)}) collective-permute-start(bf16[1,16,2,1024]{3,2,1,0:T(2,128)(2,1)} %get-tuple-element.73), channel_id=1, source_target_pairs={{0,16},{16,32},{32,48},{48,64},{64,80},{80,96},{96,112},{112,128},... | collective-permute-start | bytes 196616 | tf_op jit(solution)/shard_map/ppermute | solution.py:17
  70.5 5.9 %collective-permute-start.5 = (bf16[1,16,2,1024]{3,2,1,0:T(2,128)(2,1)}, bf16[1,16,2,1024]{3,2,1,0:T(2,128)(2,1)}, u32[]{:S(2)}, u32[]{:S(2)}) collective-permute-start(bf16[1,16,2,1024]{3,2,1,0:T(2,128)(2,1)} %get-tuple-element.74), channel_id=1, source_target_pairs={{16,0},{32,16},{48,32},{64,48},{80,64},{96,80},{112,96},{128,112},... | collective-permute-start | bytes 196616 | tf_op jit(solution)/shard_map/ppermute | solution.py:19
  77.3 9.2 %collective-permute-start.6 = (bf16[18,1,2,1024]{3,2,1,0:T(2,128)(2,1)S(1)}, bf16[18,1,2,1024]{3,2,1,0:T(2,128)(2,1)S(1)}, u32[]{:S(2)}, u32[]{:S(2)}) collective-permute-start(bf16[18,1,2,1024]{3,2,1,0:T(2,128)(2,1)S(1)} %get-tuple-element.69), channel_id=1, source_target_pairs={{0,1},{1,2},{2,3},{3,4},{4,5},{5,6},{6,7},{7,8},{8,9},{9,10},{10,1... | collective-permute-start | bytes 221192 | tf_op jit(solution)/shard_map/ppermute | solution.py:17
  80.6 6.0 %collective-permute-start.7 = (bf16[18,1,2,1024]{3,2,1,0:T(2,128)(2,1)S(1)}, bf16[18,1,2,1024]{3,2,1,0:T(2,128)(2,1)S(1)}, u32[]{:S(2)}, u32[]{:S(2)}) collective-permute-start(bf16[18,1,2,1024]{3,2,1,0:T(2,128)(2,1)S(1)} %get-tuple-element.70), channel_id=1, source_target_pairs={{1,0},{2,1},{3,2},{4,3},{5,4},{6,5},{7,6},{8,7},{9,8},{10,9},{11,1... | collective-permute-start | bytes 221192 | tf_op jit(solution)/shard_map/ppermute | solution.py:19
  244.9 93.4 %copy-start.1 = (bf16[64,64]{1,0:T(8,128)(2,1)S(1)}, bf16[64,64]{1,0:T(8,128)(2,1)}, u32[]{:S(2)}) copy-start(bf16[64,64]{1,0:T(8,128)(2,1)} %param.10) | copy-start | bytes 24580
  (33 other events, 188.3 us)
where the time goes:
time: 344 us; the launch traced here: 339 us
  other arithmetic  105 us (31%)
  local copies, waits for them, and re-layouts  104 us (30%)
  blocking collectives  83.8 us (24%)
  starting transfers between devices  23.1 us (7%)
  matrix products  15.7 us (5%)
  waiting for transfers between devices  5.02 us (1%)
    psum x1, blocking collectives, shards(): lax.psum((grad_taps_part, grad_mix_part, grad_gain_part), ('gx', 'gy'))  83.8 us
    reshape x27, local copies, waits for them, and re-layouts, tap_grads(): rows_out.append(jnp.sum((shifted * grads).reshape(-1, channels), axis=0))  76.3 us
    reduce_sum x27, other arithmetic, tap_grads(): rows_out.append(jnp.sum((shifted * grads).reshape(-1, channels), axis=0))  57.9 us
    mul x4, other arithmetic, tap_grads(): rows_out.append(jnp.sum((shifted * grads).reshape(-1, channels), axis=0))  16.6 us
    ppermute x4, starting transfers between devices, extended_2(): lax.ppermute(tail, axis, [(i, (i + 1) % count) for i in range(ends)])  16.5 us
    dot_general x2, matrix products, slot_slabs(): jnp.einsum('xypf,skp->xyskf', level_pad, select.astype(jnp.bfloat16), pre...  9.5 us
    mul x1, other arithmetic, norm_forward(): mean_square = jnp.mean(depth_slots * depth_slots, axis=-1, keepdims=True)  9.4 us
    unnamed x1, other arithmetic  9.25 us
  transfers between devices with their start and end apart: 8, of which 2 were waited for; matrix products, arithmetic and copies ran while one was open for 4% of the time, Pallas kernels for 0%

commit v1 on v0

v1 whole, which is shorter than its diff:
```python
import functools

import jax
import jax.numpy as jnp
from jax import lax
from jax.experimental import pallas as pl
from jax.experimental.pallas import tpu as pltpu
from jax.sharding import PartitionSpec as P

EPS = 1e-05
MESH = pl.DeviceIdType.MESH
F32 = jnp.float32
BF16 = jnp.bfloat16
SIDE = 16
CH = 64
KT = 8
LANES = KT * 128
ROWS = 32
SLOT = KT * ROWS
FIELD = (SIDE + 2) * SLOT
Y0 = 8
OFFSETS = (-1, 0, 1)


def zrow(oz, slot, tile):
    return oz * FIELD + slot * SLOT + tile * ROWS


def shifted_tiles(tiles, low):
    count = len(tiles)
    rot = [pltpu.roll(tile, CH, 1) for tile in tiles]
    down = [jnp.where(low, rot[k - 1], rot[k]) for k in range(count)]
    up = [jnp.where(low, rot[k], rot[(k + 1) % count]) for k in range(count)]
    return down, up


def fill_own(src, field, low):
    @pl.loop(0, SIDE)
    def _(x):
        tiles = [src[x, :, k * 128 : (k + 1) * 128].astype(F32) for k in range(KT)]
        down, up = shifted_tiles(tiles, low)
        down[0] = jnp.where(low, 0.0, down[0])
        up[-1] = jnp.where(low, up[-1], 0.0)
        for oz, values in enumerate((down, tiles, up)):
            rows = field.at[pl.ds(pl.multiple_of(oz * FIELD + (x + 1) * SLOT, SLOT), SLOT)]
            for k in range(KT):
                rows[k * ROWS + Y0 : k * ROWS + Y0 + SIDE, :] = values[k]


def gather_edges(field, ysend, csend):
    for side in range(2):
        row = Y0 + side * (SIDE - 1)
        for k in range(KT):
            column = field[pl.ds(zrow(1, 1, k) + row, SIDE, stride=SLOT), :]
            ysend[side, :, k * 128 : (k + 1) * 128] = column.astype(BF16)
    for hx in range(2):
        for hy in range(2):
            start = zrow(1, 1 + hx * (SIDE - 1), 0) + Y0 + hy * (SIDE - 1)
            csend[2 * hx + hy] = field[pl.ds(start, KT, stride=ROWS), :]


def fill_halo(field, xrecv, yrecv, crecv, masks, low):
    def masked(tiles, mask):
        same, below, above = mask
        down, up = shifted_tiles(tiles, low)
        first = jnp.where(low, below, same)
        last = jnp.where(low, same, above)
        down = [v * (first if k == 0 else same) for k, v in enumerate(down)]
        up = [v * (last if k == KT - 1 else same) for k, v in enumerate(up)]
        return down, [v * same for v in tiles], up

    for side in range(2):
        tiles = [xrecv[side, :, k * 128 : (k + 1) * 128].astype(F32) for k in range(KT)]
        for oz, values in enumerate(masked(tiles, masks[(2 * side - 1, 0)])):
            for k in range(KT):
                start = zrow(oz, side * (SIDE + 1), k) + Y0
                field[start : start + SIDE, :] = values[k]
        tiles = [yrecv[side, :, k * 128 : (k + 1) * 128].astype(F32) for k in range(KT)]
        for oz, values in enumerate(masked(tiles, masks[(0, 2 * side - 1)])):
            for k in range(KT):
                start = zrow(oz, 1, k) + (Y0 - 1, Y0 + SIDE)[side]
                field[pl.ds(start, SIDE, stride=SLOT), :] = values[k]
    low8 = low[:KT]
    row8 = lax.broadcasted_iota(jnp.int32, (KT, 128), 0)
    for hx in range(2):
        for hy in range(2):
            same, below, above = masks[(2 * hx - 1, 2 * hy - 1)]
            cell = crecv[2 * hx + hy]
            rot = pltpu.roll(cell, CH, 1)
            down = jnp.where(low8, pltpu.roll(rot, 1, 0), rot)
            up = jnp.where(low8, rot, pltpu.roll(rot, KT - 1, 0))
            down = down * jnp.where(low8 & (row8 == 0), below, same)
            up = up * jnp.where((~low8) & (row8 == KT - 1), above, same)
            for oz, value in enumerate((down, cell * same, up)):
                start = zrow(oz, hx * (SIDE + 1), 0) + (Y0 - 1, Y0 + SIDE)[hy]
                field[pl.ds(start, KT, stride=ROWS), :] = value


def stencil(field, weights, result, finish=None):
    @pl.loop(0, KT)
    def _(k):
        rows = field.at[pl.ds(pl.multiple_of(k * ROWS, ROWS), 3 * FIELD - (KT - 1) * ROWS)]
        for half in range(2):
            sums = {}
            for slot in range(SIDE + 2):
                for oz in OFFSETS:
                    for oy in OFFSETS:
                        start = (oz + 1) * FIELD + slot * SLOT + Y0 + 8 * half + oy
                        value = rows[start : start + 8, :]
                        for ox in OFFSETS:
                            x = slot - 1 - ox
                            if 0 <= x < SIDE:
                                term = value * weights[9 * (ox + 1) + 3 * (oy + 1) + oz + 1]
                                sums[x] = sums[x] + term if x in sums else term
                if slot >= 2:
                    result[slot - 2, k, 8 * half : 8 * half + 8, :] = sums.pop(slot - 2)
        if finish is not None:
            finish(k)


def tap_products(field, grads):
    def body(k, totals):
        totals = list(totals)
        span = FIELD - (KT - 1) * ROWS
        base = pl.multiple_of(k * ROWS, ROWS)
        rows = field.at[pl.ds(base, 2 * FIELD + span)]
        centre = grads.at[pl.ds(base + FIELD, span)]
        for half in range(2):
            for slot in range(SIDE + 2):
                near = {}
                for ox in OFFSETS:
                    x = slot - 1 - ox
                    if 0 <= x < SIDE:
                        start = (x + 1) * SLOT + Y0 + 8 * half
                        near[ox] = centre[start : start + 8, :]
                for oz in OFFSETS:
                    for oy in OFFSETS:
                        start = (oz + 1) * FIELD + slot * SLOT + Y0 + 8 * half + oy
                        value = rows[start : start + 8, :]
                        for ox, grad in near.items():
                            tap = 9 * (ox + 1) + 3 * (oy + 1) + oz + 1
                            totals[tap] = totals[tap] + value * grad
        return tuple(totals)

    zero = jnp.zeros((8, 128), F32)
    return lax.fori_loop(0, KT, body, (zero,) * 27)


def kernel(
    n_gx, n_gy,
    feat_hbm, map_ref, taps_ref, gain_ref, mix_ref, cot_hbm,
    mixed_hbm, gf_hbm, gt_ref, gg_ref, gm_ref,
    feat, cot, mixed, gf, gd, field, gfield, depth, tapsb, wdiag, mixacc, gainacc,
    xrecv1, yrecv1, crecv1, xrecv2, yrecv2, crecv2, ysend, csend, ysend2, csend2,
    pbuf, red, recv1, part2, recv2, part3, gath,
    io_sem, send1, land1, send2, land2, rsend, rland,
):
    gx = lax.axis_index("gx")
    gy = lax.axis_index("gy")

    load_feat = pltpu.make_async_copy(feat_hbm, feat, io_sem.at[0])
    load_cot = pltpu.make_async_copy(cot_hbm, cot, io_sem.at[1])
    load_feat.start()
    load_cot.start()

    def peer_x(d):
        return lax.rem(gx + d + n_gx, n_gx)

    def peer_y(d):
        return lax.rem(gy + d + n_gy, n_gy)

    barrier = pltpu.get_barrier_semaphore()

    @pl.loop(1, n_gx)
    def _(d):
        pl.semaphore_signal(barrier, inc=1, device_id=(peer_x(d), gy), device_id_type=MESH)

    @pl.loop(1, n_gy)
    def _(d):
        pl.semaphore_signal(barrier, inc=1, device_id=(gx, peer_y(d)), device_id_type=MESH)

    for dx in (-1, 1):
        for dy in (-1, 1):
            pl.semaphore_signal(
                barrier, inc=1, device_id=(peer_x(dx), peer_y(dy)), device_id_type=MESH
            )

    low = lax.broadcasted_iota(jnp.int32, (SIDE, 128), 1) < CH
    low8 = low[:8]

    def level(i, j):
        return jnp.where(map_ref[i, j, 1] == 0, 1, 0)

    own_level = level(gx, gy)
    masks = {}
    for dx in OFFSETS:
        for dy in OFFSETS:
            if dx == 0 and dy == 0:
                continue
            inside = (gx + dx >= 0) & (gx + dx < n_gx) & (gy + dy >= 0) & (gy + dy < n_gy)
            delta = level(peer_x(dx), peer_y(dy)) - own_level
            masks[(dx, dy)] = tuple(
                jnp.where(inside & (delta == step), 1.0, 0.0).astype(F32) for step in (0, -1, 1)
            )

    taps2 = jnp.concatenate([taps_ref[...], taps_ref[...]], axis=1)
    for tap in range(27):
        tapsb[8 * tap : 8 * tap + 8, :] = jnp.broadcast_to(taps2[tap : tap + 1, :], (8, 128))
    gain2 = jnp.concatenate([gain_ref[...], gain_ref[...]], axis=1)
    gain4 = jnp.concatenate([gain2, gain2], axis=1)
    row_block = lax.broadcasted_iota(jnp.int32, (4 * CH, 4 * CH), 0) // CH
    col_block = lax.broadcasted_iota(jnp.int32, (4 * CH, 4 * CH), 1) // CH
    diagonal = row_block == col_block
    wide = jnp.concatenate([mix_ref[...].astype(F32)] * 2, axis=1)
    wide = jnp.concatenate([wide, wide], axis=1)
    wide = jnp.concatenate([wide] * 4, axis=0)
    wdiag[0] = jnp.where(diagonal, wide, 0.0).astype(BF16)
    wdiag[1] = jnp.where(diagonal, 1.0 / CH, 0.0).astype(BF16)
    mixacc[...] = jnp.zeros_like(mixacc)
    gainacc[...] = jnp.zeros_like(gainacc)

    load_feat.wait()
    fill_own(feat, field, low)
    gather_edges(field, ysend, csend)

    def halo_copies(src, ys, cs, xr, yr, cr, send, land):
        copies = []
        for step in (-1, 1):
            far = (step + 1) // 2
            copies.append((src.at[far * (SIDE - 1)], xr.at[1 - far], (peer_x(step), gy)))
            copies.append((ys.at[far], yr.at[1 - far], (gx, peer_y(step))))
        for dx in (-1, 1):
            for dy in (-1, 1):
                here = (dx + 1) + (dy + 1) // 2
                copies.append((cs.at[here], cr.at[3 - here], (peer_x(dx), peer_y(dy))))
        return [
            pltpu.make_async_remote_copy(
                src_ref=a, dst_ref=b, send_sem=send.at[n], recv_sem=land.at[n],
                device_id=to, device_id_type=MESH,
            )
            for n, (a, b, to) in enumerate(copies)
        ]

    pl.semaphore_wait(barrier, (n_gx - 1) + (n_gy - 1) + 4)
    halo1 = halo_copies(feat, ysend, csend, xrecv1, yrecv1, crecv1, send1, land1)
    for copy in halo1:
        copy.start()
    for copy in halo1:
        copy.wait()
    fill_halo(field, xrecv1, yrecv1, crecv1, masks, low)

    weights = [tapsb[8 * tap : 8 * tap + 8, :] for tap in range(27)]
    stencil(field, weights, depth)

    load_cot.wait()
    cells = SIDE * SIDE

    @pl.loop(0, KT // 2)
    def _(m):
        lanes = pl.ds(pl.multiple_of(m * 256, 256), 256)
        values = jnp.concatenate(
            [depth[:, 2 * m + h].reshape(cells, 128) for h in range(2)], axis=1
        )
        mean_square = jnp.dot((values * values).astype(BF16), wdiag[1], preferred_element_type=F32)
        inv_rms = lax.rsqrt(mean_square + EPS)
        normed = values * inv_rms
        norm_bf = (normed * gain4).astype(BF16)
        branch = jnp.dot(norm_bf, wdiag[0], preferred_element_type=F32)
        inputs = feat[:, :, lanes].reshape(cells, 256).astype(F32)
        mixed[:, :, lanes] = (inputs + branch).astype(BF16).reshape(SIDE, SIDE, 256)
        grad_out = cot[:, :, lanes].reshape(cells, 256)
        grad_norm = lax.dot_general(
            grad_out, wdiag[0], (((1,), (1,)), ((), ())), preferred_element_type=F32
        )
        product = grad_norm * normed
        gainacc[...] += jnp.sum(product.reshape(cells // 8, 8, 256), axis=0)
        mean = jnp.dot((product * gain4).astype(BF16), wdiag[1], preferred_element_type=F32)
        grad_depth = inv_rms * (grad_norm * gain4 - normed * mean)
        gd[:, :, lanes] = grad_depth.astype(BF16).reshape(SIDE, SIDE, 256)
        mixacc[...] += lax.dot_general(
            norm_bf, grad_out, (((0,), (0,)), ((), ())), preferred_element_type=F32
        )

    store_mixed = pltpu.make_async_copy(mixed, mixed_hbm, io_sem.at[2])
    store_mixed.start()

    fill_own(gd, gfield, low)
    gather_edges(gfield, ysend2, csend2)
    halo2 = halo_copies(gd, ysend2, csend2, xrecv2, yrecv2, crecv2, send2, land2)
    for copy in halo2:
        copy.start()

    totals = list(tap_products(field, gfield))
    totals.append(gainacc[:, :128] + gainacc[:, 128:])
    folded = [total + pltpu.roll(total, CH, 1) for total in totals]
    for j in range(14):
        pair = jnp.where(low8, folded[2 * j], folded[2 * j + 1])
        pbuf[j : j + 1, :] = jnp.sum(pair, axis=0, keepdims=True)
    pbuf[14:16, :] = jnp.zeros((2, 128), F32)
    even = mixacc[0:CH, 0:128] + mixacc[2 * CH : 3 * CH, 128:256]
    odd = mixacc[CH : 2 * CH, 0:128] + mixacc[3 * CH : 4 * CH, 128:256]
    wide_low = lax.broadcasted_iota(jnp.int32, (CH, 128), 1) < CH
    both = jnp.where(wide_low, even, odd)
    both = both + pltpu.roll(both, CH, 1)
    pbuf[16:48, :] = jnp.where(wide_low[:32], both[:32], both[32:])

    per_peer = 48 // n_gx
    red[...] = jnp.zeros_like(red)
    for q in range(per_peer):
        red[:, q, :] = pbuf[n_gx * q : n_gx * q + n_gx, :]

    def remote(src, dst, index, to):
        return pltpu.make_async_remote_copy(
            src_ref=src, dst_ref=dst, send_sem=rsend.at[index], recv_sem=rland.at[index],
            device_id=to, device_id_type=MESH,
        )

    def landed(buffer, index):
        pltpu.make_async_copy(buffer, buffer, rland.at[index]).wait()

    @pl.loop(1, n_gx)
    def _(d):
        remote(red.at[peer_x(d)], recv1.at[d - 1], 0, (peer_x(d), gy)).start()

    landed(recv1, 0)
    part2[...] = red[gx] + jnp.sum(recv1[...], axis=0)
    recv2[gy] = part2[...]

    @pl.loop(1, n_gy)
    def _(d):
        remote(part2, recv2.at[gy], 1, (gx, peer_y(d))).start()

    for copy in halo2:
        copy.wait()
    fill_halo(gfield, xrecv2, yrecv2, crecv2, masks, low)

    def finish(k):
        lanes = pl.ds(pl.multiple_of(k * 128, 128), 128)
        for x in range(SIDE):
            total = cot[x, :, lanes].astype(F32) + depth[x, k]
            gf[x, :, lanes] = total.astype(BF16)

    stencil(gfield, weights[::-1], depth, finish)
    store_gf = pltpu.make_async_copy(gf, gf_hbm, io_sem.at[3])
    store_gf.start()

    landed(recv2.at[pl.ds(0, n_gy - 1)], 1)
    part3[...] = jnp.sum(recv2[...], axis=0)
    gath[gx] = part3[...]

    @pl.loop(1, n_gx)
    def _(d):
        remote(part3, gath.at[gx], 2, (peer_x(d), gy)).start()

    landed(gath.at[pl.ds(0, n_gx - 1)], 2)
    for q in range(per_peer):
        pbuf[n_gx * q : n_gx * q + n_gx, :] = gath[:, q, :]
    rows = pbuf[0:16, :]
    turned = pltpu.roll(rows, CH, 1)
    for tap in range(27):
        source = turned if tap % 2 else rows
        gt_ref[tap : tap + 1, :] = source[tap // 2 : tap // 2 + 1, :CH]
    gg_ref[...] = turned[13:14, :CH]
    packed = pbuf[16:48, :]
    gm_ref[0:32, :] = packed[:, :CH]
    gm_ref[32:64, :] = pltpu.roll(packed, CH, 1)[:, :CH]

    def sent(buffer, index):
        pltpu.make_async_copy(buffer, buffer, rsend.at[index]).wait()

    sent(recv1, 0)
    sent(recv2.at[pl.ds(0, n_gy - 1)], 1)
    sent(gath.at[pl.ds(0, n_gx - 1)], 2)
    store_mixed.wait()
    store_gf.wait()


def shards(n_gx, n_gy, features, slot_map, tap_weights, gain, mix_weight, cotangent):
    block = (SIDE, SIDE, LANES)
    padded = max(4, 48 // n_gx)
    vmem = pl.BlockSpec(memory_space=pltpu.VMEM)
    hbm = pl.BlockSpec(memory_space=pl.ANY)
    smem = pl.BlockSpec(memory_space=pltpu.SMEM)
    halo = [
        pltpu.VMEM((2, SIDE, LANES), BF16),
        pltpu.VMEM((2, SIDE, LANES), BF16),
        pltpu.VMEM((4, KT, 128), F32),
    ]
    mixed, grad_features, grad_taps, grad_gain, grad_mix = pl.pallas_call(
        functools.partial(kernel, n_gx, n_gy),
        out_shape=(
            jax.ShapeDtypeStruct(block, BF16),
            jax.ShapeDtypeStruct(block, BF16),
            jax.ShapeDtypeStruct((27, CH), F32),
            jax.ShapeDtypeStruct((1, CH), F32),
            jax.ShapeDtypeStruct((CH, CH), F32),
        ),
        in_specs=[hbm, smem, vmem, vmem, vmem, hbm],
        out_specs=(hbm, hbm, vmem, vmem, vmem),
        scratch_shapes=[pltpu.VMEM(block, BF16)] * 5
        + [pltpu.VMEM((3 * FIELD, 128), F32)] * 2
        + [
            pltpu.VMEM((SIDE, KT, SIDE, 128), F32),
            pltpu.VMEM((27 * 8, 128), F32),
            pltpu.VMEM((2, 4 * CH, 4 * CH), BF16),
            pltpu.VMEM((4 * CH, 4 * CH), F32),
            pltpu.VMEM((8, 4 * CH), F32),
        ]
        + halo
        + halo
        + halo[1:]
        + halo[1:]
        + [
            pltpu.VMEM((48, 128), F32),
            pltpu.VMEM((n_gx, padded, 128), F32),
            pltpu.VMEM((n_gx - 1, padded, 128), F32),
            pltpu.VMEM((padded, 128), F32),
            pltpu.VMEM((n_gy, padded, 128), F32),
            pltpu.VMEM((padded, 128), F32),
            pltpu.VMEM((n_gx, padded, 128), F32),
            pltpu.SemaphoreType.DMA((4,)),
            pltpu.SemaphoreType.DMA((8,)),
            pltpu.SemaphoreType.DMA((8,)),
            pltpu.SemaphoreType.DMA((8,)),
            pltpu.SemaphoreType.DMA((8,)),
            pltpu.SemaphoreType.DMA((3,)),
            pltpu.SemaphoreType.DMA((3,)),
        ],
        compiler_params=pltpu.CompilerParams(
            collective_id=0, has_side_effects=True, vmem_limit_bytes=48 * 1024 * 1024
        ),
        name="block_conv",
    )(
        features.reshape(block), slot_map, tap_weights, gain.reshape(1, CH), mix_weight,
        cotangent.reshape(block),
    )
    return (
        mixed.reshape(features.shape), grad_features.reshape(features.shape),
        grad_taps, grad_gain.reshape(CH), grad_mix,
    )


def solution(mesh):
    return jax.shard_map(
        functools.partial(shards, mesh.shape["gx"], mesh.shape["gy"]),
        mesh=mesh,
        in_specs=(P("gx", "gy", None, None), P(), P(), P(), P(), P("gx", "gy", None, None)),
        out_specs=(P("gx", "gy", None, None), P("gx", "gy", None, None), P(), P(), P()),
        check_vma=False,
    )
```

time: 344 us -> 48.4 us (0.14); the launches traced: 339 us -> 48.2 us
  other arithmetic: 105 us -> 0 us
  local copies, waits for them, and re-layouts: 104 us -> 6.31 us
  blocking collectives: 83.8 us -> 0 us
  Pallas kernels: 0 us -> 41.2 us
  starting transfers between devices: 23.1 us -> 0 us
  matrix products: 15.7 us -> 0 us
  waiting for transfers between devices: 5.02 us -> 0 us
    psum x1 -> x0, blocking collectives: 83.8 us -> none  [shards(): lax.psum((grad_taps_part, grad_mix_part, grad_gain_part), ('gx', 'gy'))]
    reshape x29 -> x0, local copies, waits for them, and re-layouts: 81.1 us -> none  [the longest x27 76.3 us: tap_grads(): rows_out.append(jnp.sum((shifted * grads).reshape(-1, channels), axis=0))]
    reduce_sum x29 -> x0, other arithmetic: 59.2 us -> none  [the longest x27 57.9 us: tap_grads(): rows_out.append(jnp.sum((shifted * grads).reshape(-1, channels), axis=0))]
    pallas_call x0 -> x1, Pallas kernels: none -> 41.2 us  [shards(): pl.pallas_call(functools.partial(kernel, n_gx, n_gy), out_shape=(jax.Shap...]
    mul x6 -> x0, other arithmetic: 26.1 us -> none  [the longest x4 16.6 us: tap_grads(): rows_out.append(jnp.sum((shifted * grads).reshape(-1, channels), axis=0))]
    ppermute x8 -> x0, starting transfers between devices: 23.1 us -> none  [the longest x4 16.5 us: extended_2(): lax.ppermute(tail, axis, [(i, (i + 1) % count) for i in range(ends)])]
    dot_general x5 -> x0, matrix products: 15.7 us -> none  [the longest x2 9.5 us: slot_slabs(): jnp.einsum('xypf,skp->xyskf', level_pad, select.astype(jnp.bfloat16), pre...]
    mul x33 -> x0, local copies, waits for them, and re-layouts: 10.6 us -> none  [the longest x2 4.68 us: norm_forward(): return (depth_slots * inv_rms, inv_rms)]
  transfers between devices with their start and end apart: 8 -> 0, of which waited for: 2 -> 0; matrix products, arithmetic and copies ran while one was open for 4% -> 0% of each run, Pallas kernels for 0% -> 0%
where the time goes in v1:
time: 48.4 us; the launch traced here: 48.2 us
  Pallas kernels  41.2 us (85%)
  local copies, waits for them, and re-layouts  6.31 us (13%)
  between operations  0.69 us (1%)
    pallas_call x1, Pallas kernels, shards(): pl.pallas_call(functools.partial(kernel, n_gx, n_gy), out_shape=(jax.Shap...  41.2 us
    unnamed x16, local copies, waits for them, and re-layouts  6.31 us

profile of v1, /device:TPU:1, one launch (start us, length us, event | category | flops | bytes accessed | tf_op | source)
XLA Modules:
  0.0 48.2 jit_solution(12602817057758623936)
XLA Ops:
  0.6 0.0 copy-start.2
  0.6 0.0 copy-start.3
  0.7 0.0 copy-start.4
  0.7 0.9 %copy.11.map_ref = s32[16,16,2]{2,1,0:T(8,128)S(1)} copy(s32[16,16,2]{1,2,0:T(2,128)} %param.7) | data formatting | bytes 4096 | tf_op args[1]
  1.6 0.0 copy-done.2
  1.6 0.0 copy-done.3
  1.6 0.0 copy-done.4
  1.6 0.0 copy-start
  1.6 1.0 %copy-done = bf16[16,16,1,1024]{3,1,2,0:T(8,128)(2,1)S(1)} copy-done((bf16[16,16,1,1024]{3,1,2,0:T(8,128)(2,1)S(1)}, bf16[16,16,1,1024]{3,1,2,0:T(8,128)(2,1)}, u32[]{:S(2)}) %copy-start) | copy-done | bytes 524312
  2.6 0.0 copy-start.1
  2.6 1.0 %copy-done.1 = bf16[16,16,1,1024]{3,1,2,0:T(8,128)(2,1)S(1)} copy-done((bf16[16,16,1,1024]{3,1,2,0:T(8,128)(2,1)S(1)}, bf16[16,16,1,1024]{3,1,2,0:T(8,128)(2,1)}, u32[]{:S(2)}) %copy-start.1) | copy-done | bytes 524312
  3.7 41.2 %block_conv.1 = (bf16[16,16,1024]{2,1,0:T(8,128)(2,1)S(1)}, bf16[16,16,1024]{2,1,0:T(8,128)(2,1)S(1)}, f32[27,64]{1,0:T(8,128)S(1)}, f32[1,64]{1,0:T(1,128)S(1)}, f32[64,64]{1,0:T(8,128)S(1)}) custom-call(bf16[16,16,1024]{2,1,0:T(8,128)(2,1)S(1)} %bitcast.10, s32[16,16,2]{2,1,0:T(8,128)S(1)} %copy.11.map_ref, f32[27,64]{1,0:T(8,128)S(1)} %copy-done.2, ...), custom_call_target="tpu_custom_call" | custom-call | tf_op jit(solution)/shard_map/block_conv/pallas_call | solution.py:389
  44.9 0.8 %copy.19 = bf16[16,16,1,1024]{3,1,2,0:T(8,128)(2,1)} copy(bf16[16,16,1,1024]{3,1,2,0:T(8,128)(2,1)S(1)} %bitcast.13) | data formatting | bytes 1048576
  45.7 0.8 %copy.20 = bf16[16,16,1,1024]{3,1,2,0:T(8,128)(2,1)} copy(bf16[16,16,1,1024]{3,1,2,0:T(8,128)(2,1)S(1)} %bitcast.12) | data formatting | bytes 1048576
  46.5 0.6 %copy.21 = f32[27,64]{1,0:T(8,128)} copy(f32[27,64]{1,0:T(8,128)S(1)} %get-tuple-element.27) | data formatting | bytes 13824
  47.1 0.5 %copy.22 = f32[64]{0:T(128)} copy(f32[64]{0:T(128)S(1)} %bitcast.15) | data formatting | bytes 512
  47.6 0.6 %copy.23 = f32[64,64]{1,0:T(8,128)} copy(f32[64,64]{1,0:T(8,128)S(1)} %get-tuple-element.29) | data formatting | bytes 32768
Async XLA Ops:
  0.6 0.9 %copy-start.2 = (f32[27,64]{1,0:T(8,128)S(1)}, f32[27,64]{1,0:T(8,128)}, u32[]{:S(2)}) copy-start(f32[27,64]{1,0:T(8,128)} %taps_ref.1) | copy-start | bytes 20740
  0.6 0.9 %copy-start.3 = (bf16[64,64]{1,0:T(8,128)(2,1)S(1)}, bf16[64,64]{1,0:T(8,128)(2,1)}, u32[]{:S(2)}) copy-start(bf16[64,64]{1,0:T(8,128)(2,1)} %mix_ref.1) | copy-start | bytes 24580
  0.7 0.9 %copy-start.4 = (f32[64]{0:T(128)S(1)}, f32[64]{0:T(128)}, u32[]{:S(2)}) copy-start(f32[64]{0:T(128)} %param.9) | copy-start | bytes 772
  1.6 1.0 %copy-start = (bf16[16,16,1,1024]{3,1,2,0:T(8,128)(2,1)S(1)}, bf16[16,16,1,1024]{3,1,2,0:T(8,128)(2,1)}, u32[]{:S(2)}) copy-start(bf16[16,16,1,1024]{3,1,2,0:T(8,128)(2,1)} %param.6) | copy-start | bytes 1572868
  2.6 1.0 %copy-start.1 = (bf16[16,16,1,1024]{3,1,2,0:T(8,128)(2,1)S(1)}, bf16[16,16,1,1024]{3,1,2,0:T(8,128)(2,1)}, u32[]{:S(2)}) copy-start(bf16[16,16,1,1024]{3,1,2,0:T(8,128)(2,1)} %param.11) | copy-start | bytes 1572868

commit v2 on v1

--- a/solution.py
+++ b/solution.py
@@ -148,11 +148,11 @@
 
 def kernel(
     n_gx, n_gy,
-    feat_hbm, map_ref, taps_ref, gain_ref, mix_ref, cot_hbm,
-    mixed_hbm, gf_hbm, gt_ref, gg_ref, gm_ref,
-    feat, cot, mixed, gf, gd, field, gfield, depth, tapsb, wdiag, mixacc, gainacc,
+    feat_hbm, map_ref, taps_hbm, gain_hbm, mix_hbm, cot_hbm,
+    mixed, gf, pbuf,
+    taps_ref, gain_ref, mix_ref, feat, cot, gd, field, gfield, depth, tapsb, wdiag, mixacc, gainacc,
     xrecv1, yrecv1, crecv1, xrecv2, yrecv2, crecv2, ysend, csend, ysend2, csend2,
-    pbuf, red, recv1, part2, recv2, part3, gath,
+    red, recv1, part2, recv2, part3, gath,
     io_sem, send1, land1, send2, land2, rsend, rland,
 ):
     gx = lax.axis_index("gx")
@@ -160,7 +160,15 @@
 
     load_feat = pltpu.make_async_copy(feat_hbm, feat, io_sem.at[0])
     load_cot = pltpu.make_async_copy(cot_hbm, cot, io_sem.at[1])
+    load_params = [
+        pltpu.make_async_copy(src, dst, io_sem.at[2 + n])
+        for n, (src, dst) in enumerate(
+            ((taps_hbm, taps_ref), (gain_hbm, gain_ref), (mix_hbm, mix_ref))
+        )
+    ]
     load_feat.start()
+    for copy in load_params:
+        copy.start()
     load_cot.start()
 
     def peer_x(d):
@@ -189,7 +197,7 @@
     low8 = low[:8]
 
     def level(i, j):
-        return jnp.where(map_ref[i, j, 1] == 0, 1, 0)
+        return jnp.where(map_ref[i, 1, j] == 0, 1, 0)
 
     own_level = level(gx, gy)
     masks = {}
@@ -203,6 +211,8 @@
                 jnp.where(inside & (delta == step), 1.0, 0.0).astype(F32) for step in (0, -1, 1)
             )
 
+    for copy in load_params:
+        copy.wait()
     taps2 = jnp.concatenate([taps_ref[...], taps_ref[...]], axis=1)
     for tap in range(27):
         tapsb[8 * tap : 8 * tap + 8, :] = jnp.broadcast_to(taps2[tap : tap + 1, :], (8, 128))
@@ -281,9 +291,6 @@
             norm_bf, grad_out, (((0,), (0,)), ((), ())), preferred_element_type=F32
         )
 
-    store_mixed = pltpu.make_async_copy(mixed, mixed_hbm, io_sem.at[2])
-    store_mixed.start()
-
     fill_own(gd, gfield, low)
     gather_edges(gfield, ysend2, csend2)
     halo2 = halo_copies(gd, ysend2, csend2, xrecv2, yrecv2, crecv2, send2, land2)
@@ -341,8 +348,6 @@
             gf[x, :, lanes] = total.astype(BF16)
 
     stencil(gfield, weights[::-1], depth, finish)
-    store_gf = pltpu.make_async_copy(gf, gf_hbm, io_sem.at[3])
-    store_gf.start()
 
     landed(recv2.at[pl.ds(0, n_gy - 1)], 1)
     part3[...] = jnp.sum(recv2[...], axis=0)
@@ -355,6 +360,28 @@
     landed(gath.at[pl.ds(0, n_gx - 1)], 2)
     for q in range(per_peer):
         pbuf[n_gx * q : n_gx * q + n_gx, :] = gath[:, q, :]
+    def sent(buffer, index):
+        pltpu.make_async_copy(buffer, buffer, rsend.at[index]).wait()
+
+    sent(recv1, 0)
+    sent(recv2.at[pl.ds(0, n_gy - 1)], 1)
+    sent(gath.at[pl.ds(0, n_gx - 1)], 2)
+
+
+def deliver(
+    mixed, gf, pbuf, mixed_hbm, gf_hbm, gt_hbm, gg_hbm, gm_hbm, gt_ref, gg_ref, gm_ref, sem
+):
+    copies = [
+        pltpu.make_async_copy(src, dst, sem.at[n])
+        for n, (src, dst) in enumerate(
+            (
+                (mixed, mixed_hbm), (gf, gf_hbm),
+                (gt_ref, gt_hbm), (gg_ref, gg_hbm), (gm_ref, gm_hbm),
+            )
+        )
+    ]
+    copies[0].start()
+    copies[1].start()
     rows = pbuf[0:16, :]
     turned = pltpu.roll(rows, CH, 1)
     for tap in range(27):
@@ -365,39 +392,36 @@
     gm_ref[0:32, :] = packed[:, :CH]
     gm_ref[32:64, :] = pltpu.roll(packed, CH, 1)[:, :CH]
 
-    def sent(buffer, index):
-        pltpu.make_async_copy(buffer, buffer, rsend.at[index]).wait()
-
-    sent(recv1, 0)
-    sent(recv2.at[pl.ds(0, n_gy - 1)], 1)
-    sent(gath.at[pl.ds(0, n_gx - 1)], 2)
-    store_mixed.wait()
-    store_gf.wait()
+    for copy in copies[2:]:
+        copy.start()
+    for copy in copies:
+        copy.wait()
 
 
 def shards(n_gx, n_gy, features, slot_map, tap_weights, gain, mix_weight, cotangent):
     block = (SIDE, SIDE, LANES)
     padded = max(4, 48 // n_gx)
     vmem = pl.BlockSpec(memory_space=pltpu.VMEM)
-    hbm = pl.BlockSpec(memory_space=pl.ANY)
+    hbm = pl.BlockSpec(memory_space=pltpu.HBM)
     smem = pl.BlockSpec(memory_space=pltpu.SMEM)
     halo = [
         pltpu.VMEM((2, SIDE, LANES), BF16),
         pltpu.VMEM((2, SIDE, LANES), BF16),
         pltpu.VMEM((4, KT, 128), F32),
     ]
-    mixed, grad_features, grad_taps, grad_gain, grad_mix = pl.pallas_call(
+    mixed, grad_features, sums = pl.pallas_call(
         functools.partial(kernel, n_gx, n_gy),
         out_shape=(
             jax.ShapeDtypeStruct(block, BF16),
             jax.ShapeDtypeStruct(block, BF16),
-            jax.ShapeDtypeStruct((27, CH), F32),
-            jax.ShapeDtypeStruct((1, CH), F32),
-            jax.ShapeDtypeStruct((CH, CH), F32),
+            jax.ShapeDtypeStruct((48, 128), F32),
         ),
-        in_specs=[hbm, smem, vmem, vmem, vmem, hbm],
-        out_specs=(hbm, hbm, vmem, vmem, vmem),
-        scratch_shapes=[pltpu.VMEM(block, BF16)] * 5
+        in_specs=[hbm, smem, hbm, hbm, hbm, hbm],
+        out_specs=(vmem, vmem, vmem),
+        scratch_shapes=[
+            pltpu.VMEM((27, CH), F32), pltpu.VMEM((1, CH), F32), pltpu.VMEM((CH, CH), BF16)
+        ]
+        + [pltpu.VMEM(block, BF16)] * 3
         + [pltpu.VMEM((3 * FIELD, 128), F32)] * 2
         + [
             pltpu.VMEM((SIDE, KT, SIDE, 128), F32),
@@ -411,14 +435,13 @@
         + halo[1:]
         + halo[1:]
         + [
-            pltpu.VMEM((48, 128), F32),
             pltpu.VMEM((n_gx, padded, 128), F32),
             pltpu.VMEM((n_gx - 1, padded, 128), F32),
             pltpu.VMEM((padded, 128), F32),
             pltpu.VMEM((n_gy, padded, 128), F32),
             pltpu.VMEM((padded, 128), F32),
             pltpu.VMEM((n_gx, padded, 128), F32),
-            pltpu.SemaphoreType.DMA((4,)),
+            pltpu.SemaphoreType.DMA((5,)),
             pltpu.SemaphoreType.DMA((8,)),
             pltpu.SemaphoreType.DMA((8,)),
             pltpu.SemaphoreType.DMA((8,)),
@@ -427,13 +450,36 @@
             pltpu.SemaphoreType.DMA((3,)),
         ],
         compiler_params=pltpu.CompilerParams(
-            collective_id=0, has_side_effects=True, vmem_limit_bytes=48 * 1024 * 1024
+            collective_id=0, has_side_effects=True, vmem_limit_bytes=40 * 1024 * 1024
         ),
         name="block_conv",
     )(
-        features.reshape(block), slot_map, tap_weights, gain.reshape(1, CH), mix_weight,
-        cotangent.reshape(block),
+        *(
+            pltpu.with_memory_space_constraint(value, pltpu.HBM)
+            for value in (
+                features.reshape(block), slot_map.transpose(0, 2, 1), tap_weights,
+                gain.reshape(1, CH), mix_weight, cotangent.reshape(block),
+            )
+        )
     )
+    mixed, grad_features, grad_taps, grad_gain, grad_mix = pl.pallas_call(
+        deliver,
+        out_shape=(
+            jax.ShapeDtypeStruct(block, BF16),
+            jax.ShapeDtypeStruct(block, BF16),
+            jax.ShapeDtypeStruct((27, CH), F32),
+            jax.ShapeDtypeStruct((1, CH), F32),
+            jax.ShapeDtypeStruct((CH, CH), F32),
+        ),
+        in_specs=[vmem] * 3,
+        out_specs=(hbm,) * 5,
+        scratch_shapes=[
+            pltpu.VMEM((27, CH), F32), pltpu.VMEM((1, CH), F32), pltpu.VMEM((CH, CH), F32),
+            pltpu.SemaphoreType.DMA((5,)),
+        ],
+        compiler_params=pltpu.CompilerParams(vmem_limit_bytes=4 * 1024 * 1024),
+        name="deliver",
+    )(mixed, grad_features, sums)
     return (
         mixed.reshape(features.shape), grad_features.reshape(features.shape),
         grad_taps, grad_gain.reshape(CH), grad_mix,

time: 48.4 us -> 41.3 us (0.85)
  local copies, waits for them, and re-layouts: 6.31 us -> 0 us
  Pallas kernels: 41.2 us -> 40.4 us
    unnamed x16 -> x0, local copies, waits for them, and re-layouts: 6.31 us -> none
    pallas_call x1, Pallas kernels: 41.2 us -> 39.4 us  [shards(): pl.pallas_call(functools.partial(kernel, n_gx, n_gy), out_shape=(jax.Shap...]
    pallas_call x0 -> x1, Pallas kernels: none -> 1.02 us  [shards(): pl.pallas_call(deliver, out_shape=(jax.ShapeDtypeStruct(block, BF16), jax...]
where the time goes in v2:
time: 41.3 us; the launch traced here: 41.1 us
  Pallas kernels  40.4 us (98%)
  between operations  0.64 us (2%)
    pallas_call x1, Pallas kernels, shards(): pl.pallas_call(functools.partial(kernel, n_gx, n_gy), out_shape=(jax.Shap...  39.4 us
    pallas_call x1, Pallas kernels, shards(): pl.pallas_call(deliver, out_shape=(jax.ShapeDtypeStruct(block, BF16), jax...  1.02 us

profile of v2, /device:TPU:1, one launch (start us, length us, event | category | flops | bytes accessed | tf_op | source)
XLA Modules:
  0.0 41.1 jit_solution(6727007595785441514)
XLA Ops:
  0.6 39.4 %block_conv.1 = (bf16[16,16,1024]{2,1,0:T(8,128)(2,1)S(1)}, bf16[16,16,1024]{2,1,0:T(8,128)(2,1)S(1)}, f32[48,128]{1,0:T(8,128)S(1)}) custom-call(bf16[16,16,1024]{2,1,0:T(8,128)(2,1)} %bitcast.11, s32[16,2,16]{2,1,0:T(2,128)} %bitcast.13, f32[27,64]{1,0:T(8,128)} %taps_hbm.1, f32[1,64]{1,0:T(1,128)} %bitcast.14, bf16[64,64]{1,0:T(8,128)(2,1)} %mix_hbm.1, ...), custom_call_target="tpu_custom_call" | custom-call | tf_op jit(solution)/shard_map/block_conv/pallas_call | solution.py:412
  40.1 1.0 %deliver.1 = (bf16[16,16,1024]{2,1,0:T(8,128)(2,1)}, bf16[16,16,1024]{2,1,0:T(8,128)(2,1)}, f32[27,64]{1,0:T(8,128)}, f32[1,64]{1,0:T(1,128)}, f32[64,64]{1,0:T(8,128)}) custom-call(bf16[16,16,1024]{2,1,0:T(8,128)(2,1)S(1)} %get-tuple-element.13.mixed, bf16[16,16,1024]{2,1,0:T(8,128)(2,1)S(1)} %get-tuple-element.14.gf, f32[48,128]{1,0:T(8,128)S(1)} %get-tuple-element.15.pbuf), custom_call_target="tpu_custom_call" | custom-call | tf_op jit(solution)/shard_map/deliver/pallas_call | solution.py:465

commit v3 on v2

v3 whole, which is shorter than its diff:
```python
import functools

import jax
import jax.numpy as jnp
from jax import lax
from jax.experimental import pallas as pl
from jax.experimental.pallas import tpu as pltpu
from jax.sharding import PartitionSpec as P

EPS = 1e-05
MESH = pl.DeviceIdType.MESH
F32 = jnp.float32
BF16 = jnp.bfloat16
SIDE = 16
CH = 64
KT = 8
LANES = KT * 128
ROWS = 32
SLOT = KT * ROWS
FIELD = (SIDE + 2) * SLOT
Y0 = 8
CELLS = SIDE * SIDE
OFFSETS = (-1, 0, 1)


def zrow(oz, slot, tile):
    return oz * FIELD + slot * SLOT + tile * ROWS


def shifted_tiles(tiles, low):
    count = len(tiles)
    rot = [pltpu.roll(tile, CH, 1) for tile in tiles]
    down = [jnp.where(low, rot[k - 1], rot[k]) for k in range(count)]
    up = [jnp.where(low, rot[k], rot[(k + 1) % count]) for k in range(count)]
    return down, up


def fill_own(tile_of, field, low):
    @pl.loop(0, SIDE, step=2)
    def _(first):
        for x in (first, first + 1):
            tiles = [tile_of(x, k) for k in range(KT)]
            down, up = shifted_tiles(tiles, low)
            down[0] = jnp.where(low, 0.0, down[0])
            up[-1] = jnp.where(low, up[-1], 0.0)
            for oz, values in enumerate((down, tiles, up)):
                rows = field.at[pl.ds(pl.multiple_of(oz * FIELD + (x + 1) * SLOT, SLOT), SLOT)]
                for k in range(KT):
                    rows[k * ROWS + Y0 : k * ROWS + Y0 + SIDE, :] = values[k]


def zero_halo(field, ycols):
    zero = jnp.zeros((8, 128), F32)
    for oz in range(3):
        for slot in (0, SIDE + 1):
            field[zrow(oz, slot, 0) : zrow(oz, slot, 0) + SLOT, :] = jnp.zeros((SLOT, 128), F32)

    @pl.loop(0, SIDE)
    def _(x):
        for oz in range(3):
            rows = field.at[pl.ds(pl.multiple_of(oz * FIELD + (x + 1) * SLOT, SLOT), SLOT)]
            for k in range(KT):
                rows[k * ROWS : k * ROWS + 8, :] = zero
                rows[k * ROWS + 24 : k * ROWS + 32, :] = zero

    @pl.loop(0, 6 * KT)
    def _(group):
        rows = ycols.at[pl.ds(pl.multiple_of(group * ROWS, ROWS), ROWS)]
        rows[0:8, :] = zero
        rows[24:32, :] = zero


def gather_edges(column, corner, ysend, csend):
    for side in range(2):
        for k in range(KT):
            values = column(k, side * (SIDE - 1))
            ysend[side, :, k * 128 : (k + 1) * 128] = values.astype(BF16)
    for hx in range(2):
        for hy in range(2):
            csend[2 * hx + hy] = corner(hx * (SIDE - 1), hy * (SIDE - 1))


def fill_halo(field, xrecv, yrecv, crecv, masks, low, ycols=None):
    def masked(tiles, mask):
        same, below, above = mask
        down, up = shifted_tiles(tiles, low)
        first = jnp.where(low, below, same)
        last = jnp.where(low, same, above)
        down = [v * (first if k == 0 else same) for k, v in enumerate(down)]
        up = [v * (last if k == KT - 1 else same) for k, v in enumerate(up)]
        return down, [v * same for v in tiles], up

    for side in range(2):
        tiles = [xrecv[side, :, k * 128 : (k + 1) * 128].astype(F32) for k in range(KT)]
        for oz, values in enumerate(masked(tiles, masks[(2 * side - 1, 0)])):
            for k in range(KT):
                start = zrow(oz, side * (SIDE + 1), k) + Y0
                field[start : start + SIDE, :] = values[k]
        tiles = [yrecv[side, :, k * 128 : (k + 1) * 128].astype(F32) for k in range(KT)]
        for oz, values in enumerate(masked(tiles, masks[(0, 2 * side - 1)])):
            for k in range(KT):
                start = zrow(oz, 1, k) + (Y0 - 1, Y0 + SIDE)[side]
                field[pl.ds(start, SIDE, stride=SLOT), :] = values[k]
                if ycols is not None:
                    start = ((side * 3 + oz) * KT + k) * ROWS + Y0
                    ycols[start : start + SIDE, :] = values[k]
    low8 = low[:KT]
    row8 = lax.broadcasted_iota(jnp.int32, (KT, 128), 0)
    for hx in range(2):
        for hy in range(2):
            same, below, above = masks[(2 * hx - 1, 2 * hy - 1)]
            cell = crecv[2 * hx + hy]
            rot = pltpu.roll(cell, CH, 1)
            down = jnp.where(low8, pltpu.roll(rot, 1, 0), rot)
            up = jnp.where(low8, rot, pltpu.roll(rot, KT - 1, 0))
            down = down * jnp.where(low8 & (row8 == 0), below, same)
            up = up * jnp.where((~low8) & (row8 == KT - 1), above, same)
            for oz, value in enumerate((down, cell * same, up)):
                start = zrow(oz, hx * (SIDE + 1), 0) + (Y0 - 1, Y0 + SIDE)[hy]
                field[pl.ds(start, KT, stride=ROWS), :] = value


def tap_index(ox, oy, oz):
    return 9 * (ox + 1) + 3 * (oy + 1) + oz + 1


def stencil(field, weights, result, first, last, finish=None):
    @pl.loop(first, last)
    def _(k):
        rows = field.at[pl.ds(pl.multiple_of(k * ROWS, ROWS), 3 * FIELD - (KT - 1) * ROWS)]
        out = result.at[pl.ds(pl.multiple_of(k * CELLS, CELLS), CELLS)]
        for half in range(2):
            sums = {}
            for slot in range(SIDE + 2):
                for oz in OFFSETS:
                    for oy in OFFSETS:
                        start = (oz + 1) * FIELD + slot * SLOT + Y0 + 8 * half + oy
                        value = rows[start : start + 8, :]
                        for ox in OFFSETS:
                            x = slot - 1 - ox
                            if 0 <= x < SIDE:
                                term = value * weights[tap_index(ox, oy, oz)]
                                sums[x] = sums[x] + term if x in sums else term
                if slot >= 2:
                    start = (slot - 2) * SIDE + 8 * half
                    out[start : start + 8, :] = sums.pop(slot - 2)
        if finish is not None:
            finish(k, out)


def add_halo_terms(field, ycols, weights, result):
    @pl.loop(0, KT)
    def _(k):
        rows = field.at[pl.ds(pl.multiple_of(k * ROWS, ROWS), 3 * FIELD - (KT - 1) * ROWS)]
        cols = ycols.at[pl.ds(pl.multiple_of(k * ROWS, ROWS), (5 * KT + 1) * ROWS)]
        out = result.at[pl.ds(pl.multiple_of(k * CELLS, CELLS), CELLS)]
        for side in range(2):
            step = 2 * side - 1
            for half in range(2):
                start = side * (SIDE - 1) * SIDE + 8 * half
                total = out[start : start + 8, :]
                for oz in OFFSETS:
                    for oy in OFFSETS:
                        at = (oz + 1) * FIELD + side * (SIDE + 1) * SLOT + Y0 + 8 * half + oy
                        total += rows[at : at + 8, :] * weights[tap_index(step, oy, oz)]
                out[start : start + 8, :] = total
        for side in range(2):
            step = 2 * side - 1
            for half in range(2):
                span = pl.ds(8 * half * SIDE + side * (SIDE - 1), 8, stride=SIDE)
                total = out[span, :]
                for oz in OFFSETS:
                    for ox in OFFSETS:
                        at = (side * 3 + oz + 1) * KT * ROWS + Y0 + 8 * half + ox
                        total += cols[at : at + 8, :] * weights[tap_index(ox, step, oz)]
                out[span, :] = total


def tap_products(field, grads, taps):
    def body(k, totals):
        totals = dict(zip(taps, totals))
        rows = field.at[pl.ds(pl.multiple_of(k * ROWS, ROWS), 3 * FIELD - (KT - 1) * ROWS)]
        own = grads.at[pl.ds(pl.multiple_of(k * CELLS, CELLS), CELLS)]
        for half in range(2):
            for slot in range(SIDE + 2):
                near = {}
                for ox in OFFSETS:
                    x = slot - 1 - ox
                    if 0 <= x < SIDE:
                        start = x * SIDE + 8 * half
                        near[ox] = own[start : start + 8, :]
                for oz in OFFSETS:
                    for oy in OFFSETS:
                        wanted = [ox for ox in near if (ox, oy, oz) in totals]
                        if not wanted:
                            continue
                        start = (oz + 1) * FIELD + slot * SLOT + Y0 + 8 * half + oy
                        value = rows[start : start + 8, :]
                        for ox in wanted:
                            totals[(ox, oy, oz)] = totals[(ox, oy, oz)] + value * near[ox]
        return tuple(totals[tap] for tap in taps)

    zero = jnp.zeros((8, 128), F32)
    return list(lax.fori_loop(0, KT, body, (zero,) * len(taps)))


TAPS = [(ox, oy, oz) for oz in OFFSETS for oy in OFFSETS for ox in OFFSETS]
GROUPS = (TAPS[:16], TAPS[16:])


def kernel(
    n_gx, n_gy,
    feat_hbm, map_ref, taps_hbm, gain_hbm, mix_hbm, cot_hbm,
    mixed, gf, tap_sums, mix_sums,
    taps_ref, gain_ref, mix_ref, feat, cot,
    field, gfield, depth, grads, ycols, normb, gnorm, xsend2, tapsb, wdiag, mixacc, gainacc,
    xrecv1, yrecv1, crecv1, xrecv2, yrecv2, crecv2, ysend, csend, ysend2, csend2,
    red, recv1, part2, recv2, part3, gath, tsend, trecv1, tpart, trecv2,
    io_sem, send1, land1, send2, land2, rsend, rland,
):
    gx = lax.axis_index("gx")
    gy = lax.axis_index("gy")

    load_feat = pltpu.make_async_copy(feat_hbm, feat, io_sem.at[0])
    load_cot = pltpu.make_async_copy(cot_hbm, cot, io_sem.at[1])
    load_params = [
        pltpu.make_async_copy(src, dst, io_sem.at[2 + n])
        for n, (src, dst) in enumerate(
            ((taps_hbm, taps_ref), (gain_hbm, gain_ref), (mix_hbm, mix_ref))
        )
    ]

    def peer_x(d):
        return lax.rem(gx + d + n_gx, n_gx)

    def peer_y(d):
        return lax.rem(gy + d + n_gy, n_gy)

    barrier = pltpu.get_barrier_semaphore()

    def greet(dx, dy):
        pl.semaphore_signal(
            barrier, inc=1, device_id=(peer_x(dx), peer_y(dy)), device_id_type=MESH
        )

    around = [(dx, dy) for dx in OFFSETS for dy in OFFSETS if (dx, dy) != (0, 0)]
    for dx, dy in around:
        greet(dx, dy)
    load_feat.start()
    for copy in load_params:
        copy.start()
    load_cot.start()

    @pl.loop(2, n_gx - 1)
    def _(d):
        greet(d, 0)

    @pl.loop(2, n_gy - 1)
    def _(d):
        greet(0, d)

    low = lax.broadcasted_iota(jnp.int32, (SIDE, 128), 1) < CH
    low8 = low[:8]

    def level(i, j):
        return jnp.where(map_ref[i, 1, j] == 0, 1, 0)

    own_level = level(gx, gy)
    masks = {}
    for dx, dy in around:
        inside = (gx + dx >= 0) & (gx + dx < n_gx) & (gy + dy >= 0) & (gy + dy < n_gy)
        delta = level(peer_x(dx), peer_y(dy)) - own_level
        masks[(dx, dy)] = tuple(
            jnp.where(inside & (delta == step), 1.0, 0.0).astype(F32) for step in (0, -1, 1)
        )

    load_feat.wait()
    fill_own(lambda x, k: feat[x, :, k * 128 : (k + 1) * 128].astype(F32), field, low)
    gather_edges(
        lambda k, y: field[pl.ds(zrow(1, 1, k) + Y0 + y, SIDE, stride=SLOT), :],
        lambda x, y: field[pl.ds(zrow(1, 1 + x, 0) + Y0 + y, KT, stride=ROWS), :],
        ysend, csend,
    )

    def halo_copies(src, ys, cs, xr, yr, cr, send, land):
        copies = []
        for far in range(2):
            step = 2 * far - 1
            copies.append((src(far), xr.at[1 - far], (peer_x(step), gy)))
            copies.append((ys.at[far], yr.at[1 - far], (gx, peer_y(step))))
        for dx in (-1, 1):
            for dy in (-1, 1):
                here = (dx + 1) + (dy + 1) // 2
                copies.append((cs.at[here], cr.at[3 - here], (peer_x(dx), peer_y(dy))))
        return [
            pltpu.make_async_remote_copy(
                src_ref=a, dst_ref=b, send_sem=send.at[n], recv_sem=land.at[n],
                device_id=to, device_id_type=MESH,
            )
            for n, (a, b, to) in enumerate(copies)
        ]

    pl.semaphore_wait(barrier, (n_gx - 1) + (n_gy - 1) + 4)
    halo1 = halo_copies(
        lambda far: feat.at[far * (SIDE - 1)], ysend, csend, xrecv1, yrecv1, crecv1, send1, land1
    )
    for copy in halo1:
        copy.start()

    for copy in load_params:
        copy.wait()
    taps2 = jnp.concatenate([taps_ref[...], taps_ref[...]], axis=1)
    for tap in range(27):
        tapsb[8 * tap : 8 * tap + 8, :] = jnp.broadcast_to(taps2[tap : tap + 1, :], (8, 128))
    gain2 = jnp.concatenate([gain_ref[...], gain_ref[...]], axis=1)
    gain4 = jnp.concatenate([gain2, gain2], axis=1)
    row_block = lax.broadcasted_iota(jnp.int32, (4 * CH, 4 * CH), 0) // CH
    col_block = lax.broadcasted_iota(jnp.int32, (4 * CH, 4 * CH), 1) // CH
    diagonal = row_block == col_block
    wide = jnp.concatenate([mix_ref[...].astype(F32)] * 2, axis=1)
    wide = jnp.concatenate([wide, wide], axis=1)
    wide = jnp.concatenate([wide] * 4, axis=0)
    wdiag[0] = jnp.where(diagonal, wide, 0.0).astype(BF16)
    wdiag[1] = jnp.where(diagonal, 1.0 / CH, 0.0).astype(BF16)
    mixacc[...] = jnp.zeros_like(mixacc)
    gainacc[...] = jnp.zeros_like(gainacc)
    zero_halo(field, ycols)
    weights = [tapsb[8 * tap : 8 * tap + 8, :] for tap in range(27)]
    stencil(field, weights, depth, 0, KT)
    load_cot.wait()

    def wide_lanes(m):
        return pl.ds(pl.multiple_of(m * 256, 256), 256)

    @pl.loop(0, KT // 2)
    def _(m):
        gnorm[m] = lax.dot_general(
            cot[:, :, wide_lanes(m)].reshape(CELLS, 256), wdiag[0],
            (((1,), (1,)), ((), ())), preferred_element_type=F32,
        )

    for copy in halo1:
        copy.wait_recv()
    fill_halo(field, xrecv1, yrecv1, crecv1, masks, low, ycols)
    add_halo_terms(field, ycols, weights, depth)

    @pl.loop(0, KT // 2)
    def _(m):
        lanes = wide_lanes(m)
        tiles = [pl.ds(pl.multiple_of((2 * m + h) * CELLS, CELLS), CELLS) for h in range(2)]
        values = jnp.concatenate([depth[tile, :] for tile in tiles], axis=1)
        mean_square = jnp.dot((values * values).astype(BF16), wdiag[1], preferred_element_type=F32)
        inv_rms = lax.rsqrt(mean_square + EPS)
        normed = values * inv_rms
        norm_bf = (normed * gain4).astype(BF16)
        normb[:, lanes] = norm_bf
        grad_norm = gnorm[m]
        product = grad_norm * normed
        gainacc[...] += jnp.sum(product.reshape(CELLS // 8, 8, 256), axis=0)
        mean = jnp.dot((product * gain4).astype(BF16), wdiag[1], preferred_element_type=F32)
        grad_depth = (inv_rms * (grad_norm * gain4 - normed * mean)).astype(BF16)
        for far in range(2):
            start = far * SIDE * (SIDE - 1)
            xsend2[far, :, lanes] = grad_depth[start : start + SIDE]
        for h, tile in enumerate(tiles):
            grads[tile, :] = grad_depth[:, h * 128 : (h + 1) * 128].astype(F32)
        mixacc[...] += lax.dot_general(
            norm_bf, cot[:, :, lanes].reshape(CELLS, 256),
            (((0,), (0,)), ((), ())), preferred_element_type=F32,
        )

    even = mixacc[0:CH, 0:128] + mixacc[2 * CH : 3 * CH, 128:256]
    odd = mixacc[CH : 2 * CH, 0:128] + mixacc[3 * CH : 4 * CH, 128:256]
    wide_low = lax.broadcasted_iota(jnp.int32, (CH, 128), 1) < CH
    both = jnp.where(wide_low, even, odd)
    both = both + pltpu.roll(both, CH, 1)
    packed = jnp.where(wide_low[:32], both[:32], both[32:])
    per_peer = 32 // n_gx
    for q in range(per_peer):
        red[:, q, :] = packed[n_gx * q : n_gx * q + n_gx, :]

    def remote(src, dst, index, to):
        return pltpu.make_async_remote_copy(
            src_ref=src, dst_ref=dst, send_sem=rsend.at[index], recv_sem=rland.at[index],
            device_id=to, device_id_type=MESH,
        )

    def landed(buffer, index):
        pltpu.make_async_copy(buffer, buffer, rland.at[index]).wait()

    @pl.loop(1, n_gx)
    def _(d):
        remote(red.at[peer_x(d)], recv1.at[d - 1], 0, (peer_x(d), gy)).start()

    gather_edges(
        lambda k, y: grads[pl.ds(k * CELLS + y, SIDE, stride=SIDE), :],
        lambda x, y: grads[pl.ds(x * SIDE + y, KT, stride=CELLS), :],
        ysend2, csend2,
    )
    halo2 = halo_copies(
        lambda far: xsend2.at[far], ysend2, csend2, xrecv2, yrecv2, crecv2, send2, land2
    )
    for copy in halo2:
        copy.start()

    for group, taps in enumerate(GROUPS):
        totals = tap_products(field, grads, taps)
        if group == 1:
            totals.append(gainacc[:, :128] + gainacc[:, 128:])
        for j in range(len(totals) // 2):
            pair = jnp.where(
                low8,
                totals[2 * j] + pltpu.roll(totals[2 * j], CH, 1),
                totals[2 * j + 1] + pltpu.roll(totals[2 * j + 1], CH, 1),
            )
            tsend[group, j : j + 1, :] = jnp.sum(pair, axis=0, keepdims=True)
        if group == 1:
            tsend[1, 6:8, :] = jnp.zeros((2, 128), F32)
        trecv1[group, gx] = tsend[group]

        @pl.loop(1, n_gx)
        def _(d):
            remote(tsend.at[group], trecv1.at[group, gx], 3 + group, (peer_x(d), gy)).start()

    fill_own(
        lambda x, k: grads[pl.ds(pl.multiple_of(k * CELLS + x * SIDE, SIDE), SIDE), :],
        gfield, low,
    )

    @pl.loop(0, KT // 2)
    def _(m):
        lanes = wide_lanes(m)
        branch = jnp.dot(normb[:, lanes], wdiag[0], preferred_element_type=F32)
        inputs = feat[:, :, lanes].reshape(CELLS, 256).astype(F32)
        mixed[:, :, lanes] = (inputs + branch).astype(BF16).reshape(SIDE, SIDE, 256)

    landed(recv1, 0)
    part2[...] = red[gx] + jnp.sum(recv1[...], axis=0)
    recv2[gy] = part2[...]

    @pl.loop(1, n_gy)
    def _(d):
        remote(part2, recv2.at[gy], 1, (gx, peer_y(d))).start()

    for copy in halo2:
        copy.wait_recv()
    fill_halo(gfield, xrecv2, yrecv2, crecv2, masks, low)

    def finish(k, out):
        lanes = pl.ds(pl.multiple_of(k * 128, 128), 128)
        for x in range(SIDE):
            total = cot[x, :, lanes].astype(F32) + out[x * SIDE : (x + 1) * SIDE, :]
            gf[x, :, lanes] = total.astype(BF16)

    stencil(gfield, weights[::-1], depth, 0, KT // 2, finish)
    for group in range(2):
        landed(trecv1.at[group, pl.ds(0, n_gx - 1)], 3 + group)
        tpart[group] = jnp.sum(trecv1[group], axis=0)
        trecv2[group, gy] = tpart[group]

        @pl.loop(1, n_gy)
        def _(d):
            remote(tpart.at[group], trecv2.at[group, gy], 5 + group, (gx, peer_y(d))).start()

    stencil(gfield, weights[::-1], depth, KT // 2, KT, finish)
    landed(recv2.at[pl.ds(0, n_gy - 1)], 1)
    part3[...] = jnp.sum(recv2[...], axis=0)
    gath[gx] = part3[...]

    @pl.loop(1, n_gx)
    def _(d):
        remote(part3, gath.at[gx], 2, (peer_x(d), gy)).start()

    def sent(buffer, index):
        pltpu.make_async_copy(buffer, buffer, rsend.at[index]).wait()

    for copy in halo1 + halo2:
        copy.wait_send()
    sent(recv1, 0)
    sent(recv2.at[pl.ds(0, n_gy - 1)], 1)
    for group in range(2):
        sent(trecv1.at[group, pl.ds(0, n_gx - 1)], 3 + group)
        landed(trecv2.at[group, pl.ds(0, n_gy - 1)], 5 + group)
        tap_sums[group] = jnp.sum(trecv2[group], axis=0)
        sent(trecv2.at[group, pl.ds(0, n_gy - 1)], 5 + group)
    landed(gath.at[pl.ds(0, n_gx - 1)], 2)
    for q in range(per_peer):
        mix_sums[n_gx * q : n_gx * q + n_gx, :] = gath[:, q, :]
    sent(gath.at[pl.ds(0, n_gx - 1)], 2)


def deliver(
    mixed, gf, tap_sums, mix_sums, mixed_hbm, gf_hbm, gt_hbm, gg_hbm, gm_hbm,
    gt_ref, gg_ref, gm_ref, sem,
):
    copies = [
        pltpu.make_async_copy(src, dst, sem.at[n])
        for n, (src, dst) in enumerate(
            (
                (mixed, mixed_hbm), (gf, gf_hbm),
                (gt_ref, gt_hbm), (gg_ref, gg_hbm), (gm_ref, gm_hbm),
            )
        )
    ]
    copies[0].start()
    copies[1].start()
    for group, taps in enumerate(GROUPS):
        rows = tap_sums[group]
        turned = pltpu.roll(rows, CH, 1)
        for place, tap in enumerate(taps):
            source = turned if place % 2 else rows
            row = tap_index(*tap)
            gt_ref[row : row + 1, :] = source[place // 2 : place // 2 + 1, :CH]
        if group == 1:
            gg_ref[...] = turned[5:6, :CH]
    gm_ref[0:32, :] = mix_sums[:, :CH]
    gm_ref[32:64, :] = pltpu.roll(mix_sums[...], CH, 1)[:, :CH]
    for copy in copies[2:]:
        copy.start()
    for copy in copies:
        copy.wait()


def shards(n_gx, n_gy, features, slot_map, tap_weights, gain, mix_weight, cotangent):
    block = (SIDE, SIDE, LANES)
    vmem = pl.BlockSpec(memory_space=pltpu.VMEM)
    hbm = pl.BlockSpec(memory_space=pltpu.HBM)
    smem = pl.BlockSpec(memory_space=pltpu.SMEM)
    halo = [
        pltpu.VMEM((2, SIDE, LANES), BF16),
        pltpu.VMEM((2, SIDE, LANES), BF16),
        pltpu.VMEM((4, KT, 128), F32),
    ]
    sums = (jax.ShapeDtypeStruct((2, 8, 128), F32), jax.ShapeDtypeStruct((32, 128), F32))
    share = 32 // n_gx
    mixed, grad_features, tap_sums, mix_sums = pl.pallas_call(
        functools.partial(kernel, n_gx, n_gy),
        out_shape=(
            jax.ShapeDtypeStruct(block, BF16), jax.ShapeDtypeStruct(block, BF16), *sums
        ),
        in_specs=[hbm, smem, hbm, hbm, hbm, hbm],
        out_specs=(vmem,) * 4,
        scratch_shapes=[
            pltpu.VMEM((27, CH), F32), pltpu.VMEM((1, CH), F32), pltpu.VMEM((CH, CH), BF16),
            pltpu.VMEM(block, BF16),
            pltpu.VMEM(block, BF16),
            pltpu.VMEM((3 * FIELD, 128), F32),
            pltpu.VMEM((3 * FIELD, 128), F32),
            pltpu.VMEM((KT * CELLS, 128), F32),
            pltpu.VMEM((KT * CELLS, 128), F32),
            pltpu.VMEM((6 * KT * ROWS, 128), F32),
            pltpu.VMEM((CELLS, LANES), BF16),
            pltpu.VMEM((4, CELLS, 256), F32),
            pltpu.VMEM((2, SIDE, LANES), BF16),
            pltpu.VMEM((27 * 8, 128), F32),
            pltpu.VMEM((2, 4 * CH, 4 * CH), BF16),
            pltpu.VMEM((4 * CH, 4 * CH), F32),
            pltpu.VMEM((8, 4 * CH), F32),
        ]
        + halo
        + halo
        + halo[1:]
        + halo[1:]
        + [
            pltpu.VMEM((n_gx, share, 128), F32),
            pltpu.VMEM((n_gx - 1, share, 128), F32),
            pltpu.VMEM((share, 128), F32),
            pltpu.VMEM((n_gy, share, 128), F32),
            pltpu.VMEM((share, 128), F32),
            pltpu.VMEM((n_gx, share, 128), F32),
            pltpu.VMEM((2, 8, 128), F32),
            pltpu.VMEM((2, n_gx, 8, 128), F32),
            pltpu.VMEM((2, 8, 128), F32),
            pltpu.VMEM((2, n_gy, 8, 128), F32),
            pltpu.SemaphoreType.DMA((5,)),
            pltpu.SemaphoreType.DMA((8,)),
            pltpu.SemaphoreType.DMA((8,)),
            pltpu.SemaphoreType.DMA((8,)),
            pltpu.SemaphoreType.DMA((8,)),
            pltpu.SemaphoreType.DMA((7,)),
            pltpu.SemaphoreType.DMA((7,)),
        ],
        compiler_params=pltpu.CompilerParams(
            collective_id=0, has_side_effects=True, vmem_limit_bytes=40 * 1024 * 1024
        ),
        name="block_conv",
    )(
        *(
            pltpu.with_memory_space_constraint(value, pltpu.HBM)
            for value in (
                features.reshape(block), slot_map.transpose(0, 2, 1), tap_weights,
                gain.reshape(1, CH), mix_weight, cotangent.reshape(block),
            )
        )
    )
    mixed, grad_features, grad_taps, grad_gain, grad_mix = pl.pallas_call(
        deliver,
        out_shape=(
            jax.ShapeDtypeStruct(block, BF16),
            jax.ShapeDtypeStruct(block, BF16),
            jax.ShapeDtypeStruct((27, CH), F32),
            jax.ShapeDtypeStruct((1, CH), F32),
            jax.ShapeDtypeStruct((CH, CH), F32),
        ),
        in_specs=[vmem] * 4,
        out_specs=(hbm,) * 5,
        scratch_shapes=[
            pltpu.VMEM((27, CH), F32), pltpu.VMEM((1, CH), F32), pltpu.VMEM((CH, CH), F32),
            pltpu.SemaphoreType.DMA((5,)),
        ],
        compiler_params=pltpu.CompilerParams(vmem_limit_bytes=4 * 1024 * 1024),
        name="deliver",
    )(mixed, grad_features, tap_sums, mix_sums)
    return (
        mixed.reshape(features.shape), grad_features.reshape(features.shape),
        grad_taps, grad_gain.reshape(CH), grad_mix,
    )


def solution(mesh):
    return jax.shard_map(
        functools.partial(shards, mesh.shape["gx"], mesh.shape["gy"]),
        mesh=mesh,
        in_specs=(P("gx", "gy", None, None), P(), P(), P(), P(), P("gx", "gy", None, None)),
        out_specs=(P("gx", "gy", None, None), P("gx", "gy", None, None), P(), P(), P()),
        check_vma=False,
    )
```

time: 41.3 us -> 36.8 us (0.89)
  Pallas kernels: 40.4 us -> 35.9 us
    pallas_call x1, Pallas kernels: 39.4 us -> 34.9 us  [shards(): pl.pallas_call(functools.partial(kernel, n_gx, n_gy), out_shape=(jax.Shap...]
where the time goes in v3:
time: 36.8 us; the launch traced here: 36.6 us
  Pallas kernels  35.9 us (98%)
  between operations  0.64 us (2%)
    pallas_call x1, Pallas kernels, shards(): pl.pallas_call(functools.partial(kernel, n_gx, n_gy), out_shape=(jax.Shap...  34.9 us
    pallas_call x1, Pallas kernels, shards(): pl.pallas_call(deliver, out_shape=(jax.ShapeDtypeStruct(block, BF16), jax...  1.02 us

profile of v3, /device:TPU:1, one launch (start us, length us, event | category | flops | bytes accessed | tf_op | source)
XLA Modules:
  0.0 36.6 jit_solution(2083325653176893613)
XLA Ops:
  0.6 34.9 %block_conv.1 = (bf16[16,16,1024]{2,1,0:T(8,128)(2,1)S(1)}, bf16[16,16,1024]{2,1,0:T(8,128)(2,1)S(1)}, f32[2,8,128]{2,1,0:T(8,128)S(1)}, f32[32,128]{1,0:T(8,128)S(1)}) custom-call(bf16[16,16,1024]{2,1,0:T(8,128)(2,1)} %bitcast.11, s32[16,2,16]{2,1,0:T(2,128)} %bitcast.13, f32[27,64]{1,0:T(8,128)} %taps_hbm.1, f32[1,64]{1,0:T(1,128)} %bitcast.14, ...), custom_call_target="tpu_custom_call" | custom-call | tf_op jit(solution)/shard_map/block_conv/pallas_call | solution.py:536
  35.6 1.0 %deliver.1 = (bf16[16,16,1024]{2,1,0:T(8,128)(2,1)}, bf16[16,16,1024]{2,1,0:T(8,128)(2,1)}, f32[27,64]{1,0:T(8,128)}, f32[1,64]{1,0:T(1,128)}, f32[64,64]{1,0:T(8,128)}) custom-call(bf16[16,16,1024]{2,1,0:T(8,128)(2,1)S(1)} %get-tuple-element.14.mixed, bf16[16,16,1024]{2,1,0:T(8,128)(2,1)S(1)} %get-tuple-element.15.gf, ...), custom_call_target="tpu_custom_call" | custom-call | tf_op jit(solution)/shard_map/deliver/pallas_call | solution.py:596

commit v4 on v3

--- a/solution.py
+++ b/solution.py
@@ -80,44 +80,50 @@
             csend[2 * hx + hy] = corner(hx * (SIDE - 1), hy * (SIDE - 1))
 
 
-def fill_halo(field, xrecv, yrecv, crecv, masks, low, ycols=None):
-    def masked(tiles, mask):
-        same, below, above = mask
-        down, up = shifted_tiles(tiles, low)
-        first = jnp.where(low, below, same)
-        last = jnp.where(low, same, above)
-        down = [v * (first if k == 0 else same) for k, v in enumerate(down)]
-        up = [v * (last if k == KT - 1 else same) for k, v in enumerate(up)]
-        return down, [v * same for v in tiles], up
-
-    for side in range(2):
-        tiles = [xrecv[side, :, k * 128 : (k + 1) * 128].astype(F32) for k in range(KT)]
-        for oz, values in enumerate(masked(tiles, masks[(2 * side - 1, 0)])):
-            for k in range(KT):
-                start = zrow(oz, side * (SIDE + 1), k) + Y0
-                field[start : start + SIDE, :] = values[k]
-        tiles = [yrecv[side, :, k * 128 : (k + 1) * 128].astype(F32) for k in range(KT)]
-        for oz, values in enumerate(masked(tiles, masks[(0, 2 * side - 1)])):
-            for k in range(KT):
-                start = zrow(oz, 1, k) + (Y0 - 1, Y0 + SIDE)[side]
-                field[pl.ds(start, SIDE, stride=SLOT), :] = values[k]
-                if ycols is not None:
-                    start = ((side * 3 + oz) * KT + k) * ROWS + Y0
-                    ycols[start : start + SIDE, :] = values[k]
+def masked_shifts(tiles, mask, low):
+    same, below, above = mask
+    down, up = shifted_tiles(tiles, low)
+    first = jnp.where(low, below, same)
+    last = jnp.where(low, same, above)
+    down = [v * (first if k == 0 else same) for k, v in enumerate(down)]
+    up = [v * (last if k == KT - 1 else same) for k, v in enumerate(up)]
+    return down, [v * same for v in tiles], up
+
+
+def fill_x(field, xrecv, side, mask, low):
+    tiles = [xrecv[side, :, k * 128 : (k + 1) * 128].astype(F32) for k in range(KT)]
+    for oz, values in enumerate(masked_shifts(tiles, mask, low)):
+        for k in range(KT):
+            start = zrow(oz, side * (SIDE + 1), k) + Y0
+            field[start : start + SIDE, :] = values[k]
+
+
+def fill_y(field, yrecv, side, mask, low, ycols=None):
+    tiles = [yrecv[side, :, k * 128 : (k + 1) * 128].astype(F32) for k in range(KT)]
+    for oz, values in enumerate(masked_shifts(tiles, mask, low)):
+        for k in range(KT):
+            start = zrow(oz, 1, k) + (Y0 - 1, Y0 + SIDE)[side]
+            field[pl.ds(start, SIDE, stride=SLOT), :] = values[k]
+            if ycols is not None:
+                start = ((side * 3 + oz) * KT + k) * ROWS + Y0
+                ycols[start : start + SIDE, :] = values[k]
+
+
+def fill_corner(field, crecv, hx, hy, mask, low):
     low8 = low[:KT]
     row8 = lax.broadcasted_iota(jnp.int32, (KT, 128), 0)
-    for hx in range(2):
-        for hy in range(2):
-            same, below, above = masks[(2 * hx - 1, 2 * hy - 1)]
-            cell = crecv[2 * hx + hy]
-            rot = pltpu.roll(cell, CH, 1)
-            down = jnp.where(low8, pltpu.roll(rot, 1, 0), rot)
-            up = jnp.where(low8, rot, pltpu.roll(rot, KT - 1, 0))
-            down = down * jnp.where(low8 & (row8 == 0), below, same)
-            up = up * jnp.where((~low8) & (row8 == KT - 1), above, same)
-            for oz, value in enumerate((down, cell * same, up)):
-                start = zrow(oz, hx * (SIDE + 1), 0) + (Y0 - 1, Y0 + SIDE)[hy]
-                field[pl.ds(start, KT, stride=ROWS), :] = value
+    same, below, above = mask
+    cell = crecv[2 * hx + hy]
+    rot = pltpu.roll(cell, CH, 1)
+    down = jnp.where(low8, pltpu.roll(rot, 1, 0), rot)
+    up = jnp.where(low8, rot, pltpu.roll(rot, KT - 1, 0))
+    down = down * jnp.where(low8 & (row8 == 0), below, same)
+    up = up * jnp.where((~low8) & (row8 == KT - 1), above, same)
+    values = (down, cell * same, up)
+    for oz, value in enumerate(values):
+        start = zrow(oz, hx * (SIDE + 1), 0) + (Y0 - 1, Y0 + SIDE)[hy]
+        field[pl.ds(start, KT, stride=ROWS), :] = value
+    return values
 
 
 def tap_index(ox, oy, oz):
@@ -148,11 +154,10 @@
             finish(k, out)
 
 
-def add_halo_terms(field, ycols, weights, result):
+def add_x_terms(field, weights, result):
     @pl.loop(0, KT)
     def _(k):
         rows = field.at[pl.ds(pl.multiple_of(k * ROWS, ROWS), 3 * FIELD - (KT - 1) * ROWS)]
-        cols = ycols.at[pl.ds(pl.multiple_of(k * ROWS, ROWS), (5 * KT + 1) * ROWS)]
         out = result.at[pl.ds(pl.multiple_of(k * CELLS, CELLS), CELLS)]
         for side in range(2):
             step = 2 * side - 1
@@ -164,6 +169,13 @@
                         at = (oz + 1) * FIELD + side * (SIDE + 1) * SLOT + Y0 + 8 * half + oy
                         total += rows[at : at + 8, :] * weights[tap_index(step, oy, oz)]
                 out[start : start + 8, :] = total
+
+
+def add_y_terms(ycols, weights, result):
+    @pl.loop(0, KT)
+    def _(k):
+        cols = ycols.at[pl.ds(pl.multiple_of(k * ROWS, ROWS), (5 * KT + 1) * ROWS)]
+        out = result.at[pl.ds(pl.multiple_of(k * CELLS, CELLS), CELLS)]
         for side in range(2):
             step = 2 * side - 1
             for half in range(2):
@@ -174,6 +186,15 @@
                         at = (side * 3 + oz + 1) * KT * ROWS + Y0 + 8 * half + ox
                         total += cols[at : at + 8, :] * weights[tap_index(ox, step, oz)]
                 out[span, :] = total
+
+
+def add_corner_terms(values, hx, hy, tapsb, result):
+    span = pl.ds(hx * (SIDE - 1) * SIDE + hy * (SIDE - 1), KT, stride=CELLS)
+    total = result[span, :]
+    for oz, value in enumerate(values):
+        tap = tap_index(2 * hx - 1, 2 * hy - 1, oz - 1)
+        total += value * tapsb[8 * tap : 8 * tap + 8, :]
+    result[span, :] = total
 
 
 def tap_products(field, grads, taps):
@@ -213,9 +234,9 @@
     feat_hbm, map_ref, taps_hbm, gain_hbm, mix_hbm, cot_hbm,
     mixed, gf, tap_sums, mix_sums,
     taps_ref, gain_ref, mix_ref, feat, cot,
-    field, gfield, depth, grads, ycols, normb, gnorm, xsend2, tapsb, wdiag, mixacc, gainacc,
+    field, gfield, depth, grads, ycols, normb, gnorm, scale, xsend2, tapsb, wdiag, mixacc, gainacc,
     xrecv1, yrecv1, crecv1, xrecv2, yrecv2, crecv2, ysend, csend, ysend2, csend2,
-    red, recv1, part2, recv2, part3, gath, tsend, trecv1, tpart, trecv2,
+    msend, mrecv1, mpart, mrecv2, tsend, trecv1, tpart, trecv2,
     io_sem, send1, land1, send2, land2, rsend, rland,
 ):
     gx = lax.axis_index("gx")
@@ -339,35 +360,41 @@
             (((1,), (1,)), ((), ())), preferred_element_type=F32,
         )
 
-    for copy in halo1:
+    for far in range(2):
+        halo1[2 * far].wait_recv()
+        fill_x(field, xrecv1, 1 - far, masks[(1 - 2 * far, 0)], low)
+    add_x_terms(field, weights, depth)
+    for far in range(2):
+        halo1[2 * far + 1].wait_recv()
+        fill_y(field, yrecv1, 1 - far, masks[(0, 1 - 2 * far)], low, ycols)
+    add_y_terms(ycols, weights, depth)
+    for copy in halo1[4:]:
         copy.wait_recv()
-    fill_halo(field, xrecv1, yrecv1, crecv1, masks, low, ycols)
-    add_halo_terms(field, ycols, weights, depth)
-
-    @pl.loop(0, KT // 2)
-    def _(m):
-        lanes = wide_lanes(m)
-        tiles = [pl.ds(pl.multiple_of((2 * m + h) * CELLS, CELLS), CELLS) for h in range(2)]
-        values = jnp.concatenate([depth[tile, :] for tile in tiles], axis=1)
-        mean_square = jnp.dot((values * values).astype(BF16), wdiag[1], preferred_element_type=F32)
-        inv_rms = lax.rsqrt(mean_square + EPS)
-        normed = values * inv_rms
-        norm_bf = (normed * gain4).astype(BF16)
-        normb[:, lanes] = norm_bf
-        grad_norm = gnorm[m]
-        product = grad_norm * normed
-        gainacc[...] += jnp.sum(product.reshape(CELLS // 8, 8, 256), axis=0)
-        mean = jnp.dot((product * gain4).astype(BF16), wdiag[1], preferred_element_type=F32)
-        grad_depth = (inv_rms * (grad_norm * gain4 - normed * mean)).astype(BF16)
-        for far in range(2):
-            start = far * SIDE * (SIDE - 1)
-            xsend2[far, :, lanes] = grad_depth[start : start + SIDE]
-        for h, tile in enumerate(tiles):
-            grads[tile, :] = grad_depth[:, h * 128 : (h + 1) * 128].astype(F32)
-        mixacc[...] += lax.dot_general(
-            norm_bf, cot[:, :, lanes].reshape(CELLS, 256),
-            (((0,), (0,)), ((), ())), preferred_element_type=F32,
-        )
+    for hx in range(2):
+        for hy in range(2):
+            values = fill_corner(field, crecv1, hx, hy, masks[(2 * hx - 1, 2 * hy - 1)], low)
+            add_corner_terms(values, hx, hy, tapsb, depth)
+
+    def tiles_of(m):
+        return [pl.ds(pl.multiple_of((2 * m + h) * CELLS, CELLS), CELLS) for h in range(2)]
+
+    @pl.loop(0, KT // 2, step=2)
+    def _(first):
+        for m in (first, first + 1):
+            lanes = wide_lanes(m)
+            values = jnp.concatenate([depth[tile, :] for tile in tiles_of(m)], axis=1)
+            mean_square = jnp.dot(
+                (values * values).astype(BF16), wdiag[1], preferred_element_type=F32
+            )
+            inv_rms = lax.rsqrt(mean_square + EPS)
+            normed = values * inv_rms
+            norm_bf = (normed * gain4).astype(BF16)
+            scale[m] = inv_rms
+            normb[:, lanes] = norm_bf
+            mixacc[...] += lax.dot_general(
+                norm_bf, cot[:, :, lanes].reshape(CELLS, 256),
+                (((0,), (0,)), ((), ())), preferred_element_type=F32,
+            )
 
     even = mixacc[0:CH, 0:128] + mixacc[2 * CH : 3 * CH, 128:256]
     odd = mixacc[CH : 2 * CH, 0:128] + mixacc[3 * CH : 4 * CH, 128:256]
@@ -375,9 +402,8 @@
     both = jnp.where(wide_low, even, odd)
     both = both + pltpu.roll(both, CH, 1)
     packed = jnp.where(wide_low[:32], both[:32], both[32:])
-    per_peer = 32 // n_gx
-    for q in range(per_peer):
-        red[:, q, :] = packed[n_gx * q : n_gx * q + n_gx, :]
+    msend[...] = packed.astype(BF16)
+    mrecv1[gy] = msend[...]
 
     def remote(src, dst, index, to):
         return pltpu.make_async_remote_copy(
@@ -388,39 +414,58 @@
     def landed(buffer, index):
         pltpu.make_async_copy(buffer, buffer, rland.at[index]).wait()
 
-    @pl.loop(1, n_gx)
+    @pl.loop(1, n_gy)
     def _(d):
-        remote(red.at[peer_x(d)], recv1.at[d - 1], 0, (peer_x(d), gy)).start()
-
-    gather_edges(
-        lambda k, y: grads[pl.ds(k * CELLS + y, SIDE, stride=SIDE), :],
-        lambda x, y: grads[pl.ds(x * SIDE + y, KT, stride=CELLS), :],
-        ysend2, csend2,
-    )
-    halo2 = halo_copies(
-        lambda far: xsend2.at[far], ysend2, csend2, xrecv2, yrecv2, crecv2, send2, land2
-    )
-    for copy in halo2:
-        copy.start()
+        remote(msend, mrecv1.at[gy], 0, (gx, peer_y(d))).start()
+
+    @pl.loop(0, KT // 2, step=2)
+    def _(first):
+        for m in (first, first + 1):
+            lanes = wide_lanes(m)
+            inv_rms = scale[m]
+            values = jnp.concatenate([depth[tile, :] for tile in tiles_of(m)], axis=1)
+            normed = values * inv_rms
+            grad_norm = gnorm[m]
+            product = grad_norm * normed
+            gainacc[...] += jnp.sum(product.reshape(CELLS // 8, 8, 256), axis=0)
+            mean = jnp.dot((product * gain4).astype(BF16), wdiag[1], preferred_element_type=F32)
+            grad_depth = (inv_rms * (grad_norm * gain4 - normed * mean)).astype(BF16)
+            for far in range(2):
+                start = far * SIDE * (SIDE - 1)
+                xsend2[far, :, lanes] = grad_depth[start : start + SIDE]
+            for h, tile in enumerate(tiles_of(m)):
+                grads[tile, :] = grad_depth[:, h * 128 : (h + 1) * 128].astype(F32)
 
     for group, taps in enumerate(GROUPS):
         totals = tap_products(field, grads, taps)
         if group == 1:
             totals.append(gainacc[:, :128] + gainacc[:, 128:])
+        rows = []
         for j in range(len(totals) // 2):
             pair = jnp.where(
                 low8,
                 totals[2 * j] + pltpu.roll(totals[2 * j], CH, 1),
                 totals[2 * j + 1] + pltpu.roll(totals[2 * j + 1], CH, 1),
             )
-            tsend[group, j : j + 1, :] = jnp.sum(pair, axis=0, keepdims=True)
-        if group == 1:
-            tsend[1, 6:8, :] = jnp.zeros((2, 128), F32)
+            rows.append(jnp.sum(pair, axis=0, keepdims=True))
+        rows += [jnp.zeros((1, 128), F32)] * (8 - len(rows))
+        tsend[group] = jnp.concatenate(rows, axis=0).astype(BF16)
         trecv1[group, gx] = tsend[group]
 
         @pl.loop(1, n_gx)
         def _(d):
-            remote(tsend.at[group], trecv1.at[group, gx], 3 + group, (peer_x(d), gy)).start()
+            remote(tsend.at[group], trecv1.at[group, gx], 2 + group, (peer_x(d), gy)).start()
+
+    gather_edges(
+        lambda k, y: grads[pl.ds(k * CELLS + y, SIDE, stride=SIDE), :],
+        lambda x, y: grads[pl.ds(x * SIDE + y, KT, stride=CELLS), :],
+        ysend2, csend2,
+    )
+    halo2 = halo_copies(
+        lambda far: xsend2.at[far], ysend2, csend2, xrecv2, yrecv2, crecv2, send2, land2
+    )
+    for copy in halo2:
+        copy.start()
 
     fill_own(
         lambda x, k: grads[pl.ds(pl.multiple_of(k * CELLS + x * SIDE, SIDE), SIDE), :],
@@ -434,60 +479,52 @@
         inputs = feat[:, :, lanes].reshape(CELLS, 256).astype(F32)
         mixed[:, :, lanes] = (inputs + branch).astype(BF16).reshape(SIDE, SIDE, 256)
 
-    landed(recv1, 0)
-    part2[...] = red[gx] + jnp.sum(recv1[...], axis=0)
-    recv2[gy] = part2[...]
-
-    @pl.loop(1, n_gy)
-    def _(d):
-        remote(part2, recv2.at[gy], 1, (gx, peer_y(d))).start()
-
-    for copy in halo2:
-        copy.wait_recv()
-    fill_halo(gfield, xrecv2, yrecv2, crecv2, masks, low)
-
     def finish(k, out):
         lanes = pl.ds(pl.multiple_of(k * 128, 128), 128)
         for x in range(SIDE):
             total = cot[x, :, lanes].astype(F32) + out[x * SIDE : (x + 1) * SIDE, :]
             gf[x, :, lanes] = total.astype(BF16)
 
-    stencil(gfield, weights[::-1], depth, 0, KT // 2, finish)
+    landed(mrecv1.at[pl.ds(0, n_gy - 1)], 0)
+    mpart[...] = jnp.sum(mrecv1[...].astype(F32), axis=0).astype(BF16)
+    mrecv2[gx] = mpart[...]
+
+    @pl.loop(1, n_gx)
+    def _(d):
+        remote(mpart, mrecv2.at[gx], 1, (peer_x(d), gy)).start()
+
     for group in range(2):
-        landed(trecv1.at[group, pl.ds(0, n_gx - 1)], 3 + group)
-        tpart[group] = jnp.sum(trecv1[group], axis=0)
+        landed(trecv1.at[group, pl.ds(0, n_gx - 1)], 2 + group)
+        tpart[group] = jnp.sum(trecv1[group].astype(F32), axis=0).astype(BF16)
         trecv2[group, gy] = tpart[group]
 
         @pl.loop(1, n_gy)
         def _(d):
-            remote(tpart.at[group], trecv2.at[group, gy], 5 + group, (gx, peer_y(d))).start()
-
-    stencil(gfield, weights[::-1], depth, KT // 2, KT, finish)
-    landed(recv2.at[pl.ds(0, n_gy - 1)], 1)
-    part3[...] = jnp.sum(recv2[...], axis=0)
-    gath[gx] = part3[...]
-
-    @pl.loop(1, n_gx)
-    def _(d):
-        remote(part3, gath.at[gx], 2, (peer_x(d), gy)).start()
-
+            remote(tpart.at[group], trecv2.at[group, gy], 4 + group, (gx, peer_y(d))).start()
+
+    for copy in halo2:
+        copy.wait_recv()
+    for side in range(2):
+        fill_x(gfield, xrecv2, side, masks[(2 * side - 1, 0)], low)
+        fill_y(gfield, yrecv2, side, masks[(0, 2 * side - 1)], low)
+        for hy in range(2):
+            fill_corner(gfield, crecv2, side, hy, masks[(2 * side - 1, 2 * hy - 1)], low)
+
+    stencil(gfield, weights[::-1], depth, 0, KT, finish)
     def sent(buffer, index):
         pltpu.make_async_copy(buffer, buffer, rsend.at[index]).wait()
 
     for copy in halo1 + halo2:
         copy.wait_send()
-    sent(recv1, 0)
-    sent(recv2.at[pl.ds(0, n_gy - 1)], 1)
+    sent(mrecv1.at[pl.ds(0, n_gy - 1)], 0)
+    landed(mrecv2.at[pl.ds(0, n_gx - 1)], 1)
+    mix_sums[...] = jnp.sum(mrecv2[...].astype(F32), axis=0)
+    sent(mrecv2.at[pl.ds(0, n_gx - 1)], 1)
     for group in range(2):
-        sent(trecv1.at[group, pl.ds(0, n_gx - 1)], 3 + group)
-        landed(trecv2.at[group, pl.ds(0, n_gy - 1)], 5 + group)
-        tap_sums[group] = jnp.sum(trecv2[group], axis=0)
-        sent(trecv2.at[group, pl.ds(0, n_gy - 1)], 5 + group)
-    landed(gath.at[pl.ds(0, n_gx - 1)], 2)
-    for q in range(per_peer):
-        mix_sums[n_gx * q : n_gx * q + n_gx, :] = gath[:, q, :]
-    sent(gath.at[pl.ds(0, n_gx - 1)], 2)
-
+        sent(trecv1.at[group, pl.ds(0, n_gx - 1)], 2 + group)
+        landed(trecv2.at[group, pl.ds(0, n_gy - 1)], 4 + group)
+        tap_sums[group] = jnp.sum(trecv2[group].astype(F32), axis=0)
+        sent(trecv2.at[group, pl.ds(0, n_gy - 1)], 4 + group)
 
 def deliver(
     mixed, gf, tap_sums, mix_sums, mixed_hbm, gf_hbm, gt_hbm, gg_hbm, gm_hbm,
@@ -532,7 +569,6 @@
         pltpu.VMEM((4, KT, 128), F32),
     ]
     sums = (jax.ShapeDtypeStruct((2, 8, 128), F32), jax.ShapeDtypeStruct((32, 128), F32))
-    share = 32 // n_gx
     mixed, grad_features, tap_sums, mix_sums = pl.pallas_call(
         functools.partial(kernel, n_gx, n_gy),
         out_shape=(
@@ -551,6 +587,7 @@
             pltpu.VMEM((6 * KT * ROWS, 128), F32),
             pltpu.VMEM((CELLS, LANES), BF16),
             pltpu.VMEM((4, CELLS, 256), F32),
+            pltpu.VMEM((4, CELLS, 256), F32),
             pltpu.VMEM((2, SIDE, LANES), BF16),
             pltpu.VMEM((27 * 8, 128), F32),
             pltpu.VMEM((2, 4 * CH, 4 * CH), BF16),
@@ -562,23 +599,21 @@
         + halo[1:]
         + halo[1:]
         + [
-            pltpu.VMEM((n_gx, share, 128), F32),
-            pltpu.VMEM((n_gx - 1, share, 128), F32),
-            pltpu.VMEM((share, 128), F32),
-            pltpu.VMEM((n_gy, share, 128), F32),
-            pltpu.VMEM((share, 128), F32),
-            pltpu.VMEM((n_gx, share, 128), F32),
-            pltpu.VMEM((2, 8, 128), F32),
-            pltpu.VMEM((2, n_gx, 8, 128), F32),
-            pltpu.VMEM((2, 8, 128), F32),
-            pltpu.VMEM((2, n_gy, 8, 128), F32),
+            pltpu.VMEM((32, 128), BF16),
+            pltpu.VMEM((n_gy, 32, 128), BF16),
+            pltpu.VMEM((32, 128), BF16),
+            pltpu.VMEM((n_gx, 32, 128), BF16),
+            pltpu.VMEM((2, 8, 128), BF16),
+            pltpu.VMEM((2, n_gx, 8, 128), BF16),
+            pltpu.VMEM((2, 8, 128), BF16),
+            pltpu.VMEM((2, n_gy, 8, 128), BF16),
             pltpu.SemaphoreType.DMA((5,)),
             pltpu.SemaphoreType.DMA((8,)),
             pltpu.SemaphoreType.DMA((8,)),
             pltpu.SemaphoreType.DMA((8,)),
             pltpu.SemaphoreType.DMA((8,)),
-            pltpu.SemaphoreType.DMA((7,)),
-            pltpu.SemaphoreType.DMA((7,)),
+            pltpu.SemaphoreType.DMA((6,)),
+            pltpu.SemaphoreType.DMA((6,)),
         ],
         compiler_params=pltpu.CompilerParams(
             collective_id=0, has_side_effects=True, vmem_limit_bytes=40 * 1024 * 1024

time: 36.8 us -> 32.9 us (0.89)
  Pallas kernels: 35.9 us -> 32.1 us
    pallas_call x1, Pallas kernels: 34.9 us -> 31 us  [shards(): pl.pallas_call(functools.partial(kernel, n_gx, n_gy), out_shape=(jax.Shap...]
where the time goes in v4:
time: 32.9 us; the launch traced here: 32.7 us
  Pallas kernels  32.1 us (98%)
  between operations  0.64 us (2%)
    pallas_call x1, Pallas kernels, shards(): pl.pallas_call(functools.partial(kernel, n_gx, n_gy), out_shape=(jax.Shap...  31 us
    pallas_call x1, Pallas kernels, shards(): pl.pallas_call(deliver, out_shape=(jax.ShapeDtypeStruct(block, BF16), jax...  1.02 us

profile of v4, /device:TPU:1, one launch (start us, length us, event | category | flops | bytes accessed | tf_op | source)
XLA Modules:
  0.0 32.7 jit_solution(4544074219254289044)
XLA Ops:
  0.6 31.0 %block_conv.1 = (bf16[16,16,1024]{2,1,0:T(8,128)(2,1)S(1)}, bf16[16,16,1024]{2,1,0:T(8,128)(2,1)S(1)}, f32[2,8,128]{2,1,0:T(8,128)S(1)}, f32[32,128]{1,0:T(8,128)S(1)}) custom-call(bf16[16,16,1024]{2,1,0:T(8,128)(2,1)} %bitcast.11, s32[16,2,16]{2,1,0:T(2,128)} %bitcast.13, f32[27,64]{1,0:T(8,128)} %taps_hbm.1, f32[1,64]{1,0:T(1,128)} %bitcast.14, ...), custom_call_target="tpu_custom_call" | custom-call | tf_op jit(solution)/shard_map/block_conv/pallas_call | solution.py:572
  31.7 1.0 %deliver.1 = (bf16[16,16,1024]{2,1,0:T(8,128)(2,1)}, bf16[16,16,1024]{2,1,0:T(8,128)(2,1)}, f32[27,64]{1,0:T(8,128)}, f32[1,64]{1,0:T(1,128)}, f32[64,64]{1,0:T(8,128)}) custom-call(bf16[16,16,1024]{2,1,0:T(8,128)(2,1)S(1)} %get-tuple-element.14.mixed, bf16[16,16,1024]{2,1,0:T(8,128)(2,1)S(1)} %get-tuple-element.15.gf, ...), custom_call_target="tpu_custom_call" | custom-call | tf_op jit(solution)/shard_map/deliver/pallas_call | solution.py:631

commit v5 on v4

--- a/solution.py
+++ b/solution.py
@@ -351,7 +351,7 @@
     load_cot.wait()
 
     def wide_lanes(m):
-        return pl.ds(pl.multiple_of(m * 256, 256), 256)
+        return slice(256 * m, 256 * m + 256) if isinstance(m, int) else pl.ds(pl.multiple_of(m * 256, 256), 256)
 
     @pl.loop(0, KT // 2)
     def _(m):
@@ -376,11 +376,13 @@
             add_corner_terms(values, hx, hy, tapsb, depth)
 
     def tiles_of(m):
+        if isinstance(m, int):
+            return [slice((2 * m + h) * CELLS, (2 * m + h + 1) * CELLS) for h in range(2)]
         return [pl.ds(pl.multiple_of((2 * m + h) * CELLS, CELLS), CELLS) for h in range(2)]
 
-    @pl.loop(0, KT // 2, step=2)
+    @pl.loop(0, KT // 2, step=4)
     def _(first):
-        for m in (first, first + 1):
+        for m in range(4):
             lanes = wide_lanes(m)
             values = jnp.concatenate([depth[tile, :] for tile in tiles_of(m)], axis=1)
             mean_square = jnp.dot(
@@ -418,9 +420,9 @@
     def _(d):
         remote(msend, mrecv1.at[gy], 0, (gx, peer_y(d))).start()
 
-    @pl.loop(0, KT // 2, step=2)
+    @pl.loop(0, KT // 2, step=4)
     def _(first):
-        for m in (first, first + 1):
+        for m in range(4):
             lanes = wide_lanes(m)
             inv_rms = scale[m]
             values = jnp.concatenate([depth[tile, :] for tile in tiles_of(m)], axis=1)
@@ -495,7 +497,7 @@
 
     for group in range(2):
         landed(trecv1.at[group, pl.ds(0, n_gx - 1)], 2 + group)
-        tpart[group] = jnp.sum(trecv1[group].astype(F32), axis=0).astype(BF16)
+        tpart[group] = jnp.sum(trecv1[group].astype(F32), axis=0)
         trecv2[group, gy] = tpart[group]
 
         @pl.loop(1, n_gy)
@@ -523,7 +525,7 @@
     for group in range(2):
         sent(trecv1.at[group, pl.ds(0, n_gx - 1)], 2 + group)
         landed(trecv2.at[group, pl.ds(0, n_gy - 1)], 4 + group)
-        tap_sums[group] = jnp.sum(trecv2[group].astype(F32), axis=0)
+        tap_sums[group] = jnp.sum(trecv2[group], axis=0)
         sent(trecv2.at[group, pl.ds(0, n_gy - 1)], 4 + group)
 
 def deliver(
@@ -605,8 +607,8 @@
             pltpu.VMEM((n_gx, 32, 128), BF16),
             pltpu.VMEM((2, 8, 128), BF16),
             pltpu.VMEM((2, n_gx, 8, 128), BF16),
-            pltpu.VMEM((2, 8, 128), BF16),
-            pltpu.VMEM((2, n_gy, 8, 128), BF16),
+            pltpu.VMEM((2, 8, 128), F32),
+            pltpu.VMEM((2, n_gy, 8, 128), F32),
             pltpu.SemaphoreType.DMA((5,)),
             pltpu.SemaphoreType.DMA((8,)),
             pltpu.SemaphoreType.DMA((8,)),

time: 32.9 us -> 32.4 us (0.985)
  Pallas kernels: 32.1 us -> 31.6 us
    pallas_call x1, Pallas kernels: 31 us -> 30.6 us  [shards(): pl.pallas_call(functools.partial(kernel, n_gx, n_gy), out_shape=(jax.Shap...]
where the time goes in v5:
time: 32.4 us; the launch traced here: 32.2 us
  Pallas kernels  31.6 us (98%)
  between operations  0.64 us (2%)
    pallas_call x1, Pallas kernels, shards(): pl.pallas_call(functools.partial(kernel, n_gx, n_gy), out_shape=(jax.Shap...  30.6 us
    pallas_call x1, Pallas kernels, shards(): pl.pallas_call(deliver, out_shape=(jax.ShapeDtypeStruct(block, BF16), jax...  1.02 us

profile of v5, /device:TPU:1, one launch (start us, length us, event | category | flops | bytes accessed | tf_op | source)
XLA Modules:
  0.0 32.2 jit_solution(2279898166156067366)
XLA Ops:
  0.6 30.6 %block_conv.1 = (bf16[16,16,1024]{2,1,0:T(8,128)(2,1)S(1)}, bf16[16,16,1024]{2,1,0:T(8,128)(2,1)S(1)}, f32[2,8,128]{2,1,0:T(8,128)S(1)}, f32[32,128]{1,0:T(8,128)S(1)}) custom-call(bf16[16,16,1024]{2,1,0:T(8,128)(2,1)} %bitcast.11, s32[16,2,16]{2,1,0:T(2,128)} %bitcast.13, f32[27,64]{1,0:T(8,128)} %taps_hbm.1, f32[1,64]{1,0:T(1,128)} %bitcast.14, ...), custom_call_target="tpu_custom_call" | custom-call | tf_op jit(solution)/shard_map/block_conv/pallas_call | solution.py:574
  31.2 1.0 %deliver.1 = (bf16[16,16,1024]{2,1,0:T(8,128)(2,1)}, bf16[16,16,1024]{2,1,0:T(8,128)(2,1)}, f32[27,64]{1,0:T(8,128)}, f32[1,64]{1,0:T(1,128)}, f32[64,64]{1,0:T(8,128)}) custom-call(bf16[16,16,1024]{2,1,0:T(8,128)(2,1)S(1)} %get-tuple-element.14.mixed, bf16[16,16,1024]{2,1,0:T(8,128)(2,1)S(1)} %get-tuple-element.15.gf, ...), custom_call_target="tpu_custom_call" | custom-call | tf_op jit(solution)/shard_map/deliver/pallas_call | solution.py:633
